TPU v7x, 256 devices: a whole 4x4x8 slice. The times are simulated.
256 devices in a mesh: band: 16 (over x_hi, y, core), ga: 16 (over z, x_lo).
Axes of the slice: x: 4 (x_hi: 2, x_lo: 2; x = x_hi * 2 + x_lo), y: 4, z: 8, core: 2. Of those that a mesh axis runs over, the one named last changes fastest.
Arguments:
- coeffs: float32 [1024, 65536], P('band', 'ga'), may hold values from -90 to 90, as said below
Outputs:
- orthonormal: float32 [1024, 65536], P('band', 'ga')
Inputs may be any that keep to these rules, and one draw needn't show every extreme that they name: `coeffs`: bands are linearly independent.
All inputs are finite; a program needn't handle non-finite values.
Results may differ from a plain program's by a relative error of at most 0.00029.
Values sent between devices are 32-bit elements; how exact they have to be, the bound alone decides.
A program may use at most 128 MiB of HBM per device.

v0:
```python
import jax
import jax.numpy as jnp
from jax import lax
from jax.sharding import PartitionSpec as P


def local(coeffs):
    band_rows, width = coeffs.shape
    columns_all = width * lax.axis_size("ga")
    gathered = lax.all_gather(coeffs, "band", axis=0, tiled=True)
    partial_value = (
        jnp.dot(
            coeffs, gathered.T, precision=lax.Precision.HIGHEST, preferred_element_type=jnp.float32
        )
        / columns_all
    )
    summed = lax.psum(partial_value, "ga")
    margin = lax.all_gather(summed, "band", axis=0, tiled=True)
    factor = jnp.linalg.cholesky(margin)
    order = factor.shape[0]
    start = lax.axis_index("band") * band_rows
    row_ids = lax.broadcasted_iota(jnp.int32, (order, band_rows), 0)
    col_ids = lax.broadcasted_iota(jnp.int32, (order, band_rows), 1)
    selector = jnp.where(row_ids == col_ids + start, 1.0, 0.0).astype(jnp.float32)
    solved = lax.linalg.triangular_solve(
        factor, selector, left_side=True, lower=True, transpose_a=True
    )
    own_rows = solved.T
    return jnp.dot(
        own_rows, gathered, precision=lax.Precision.HIGHEST, preferred_element_type=jnp.float32
    )


def solution(mesh):
    return jax.shard_map(
        local,
        mesh=mesh,
        in_specs=(P("band", "ga"),),
        out_specs=P("band", "ga"),
        check_vma=False,
    )
```

profile of v0, /device:TPU:29, one launch (start us, length us, event | category | flops | bytes accessed | tf_op | source)
XLA Modules:
  0.0 697.5 jit_solution(17107480262078073157)
XLA Ops:
  6.5 0.7 all-gather.3.cloned.1.call-update
  7.3 115.8 %all-gather.3.cloned.1.call-done = f32[1024,4096]{1,0:T(8,128)} async-done(((f32[64,4096]{1,0:T(8,128)}), f32[1024,4096]{1,0:T(8,128)}) %all-gather.3.cloned.1.call-update) | async-done | bytes 16777232 | tf_op jit(solution)/shard_map/all_gather | solution.py:10
  123.1 20.5 %convolution_multiply_fusion = f32[64,1024]{1,0:T(8,128)} fusion(f32[64,4096]{1,0:T(8,128)} %param.1, f32[1024,4096]{1,0:T(8,128)} %all-gather.3.cloned.1.call-done), kind=kOutput, calls=%fused_computation.13 | convolution fusion | flops 3221291008 | bytes 18087936 | tf_op jit(solution)/shard_map/dot_general | solution.py:12
  143.7 128.0 %all-reduce.3.cloned.1.call-done = f32[64,1024]{1,0:T(8,128)} async-done(((f32[64,1024]{1,0:T(8,128)}), f32[64,1024]{1,0:T(8,128)}) %all-reduce.3.cloned.1.call-update) | async-done | bytes 262160 | tf_op jit(solution)/shard_map/psum | solution.py:17
  271.8 69.2 %all-gather.5.cloned.1.call-done = f32[1024,1024]{1,0:T(8,128)} async-done(((f32[64,1024]{1,0:T(8,128)}), f32[1024,1024]{1,0:T(8,128)}) %all-gather.5.cloned.1.call-update) | async-done | bytes 4194320 | tf_op jit(solution)/shard_map/all_gather | solution.py:18
  341.0 5.5 copy.4
  346.5 4.4 fusion
  351.0 1.9 copy-done
  352.9 11.7 %cholesky.223 = f32[128,128]{1,0:T(8,128)S(1)} custom-call(f32[128,128]{1,0:T(8,128)S(1)} %cholesky.580), custom_call_target="Cholesky" | custom-call | tf_op jit(solution)/shard_map/jit(cholesky)/cholesky | solution.py:19
  364.7 9.8 %custom-call.62 = f32[1,128,128]{1,2,0:T(8,128)S(1)} custom-call(f32[1,128,128]{2,1,0:T(8,128)S(1)} %get-tuple-element.44), custom_call_target="InvertDiagBlocksLowerTriangular" | custom-call | tf_op jit(solution)/shard_map/jit(cholesky)/cholesky | solution.py:19
  374.5 2.5 cholesky.255
  377.0 2.3 constant_dynamic-update-slice_fusion.32
  379.3 1.5 convolution_subtract_fusion
  380.9 11.9 %cholesky.244 = f32[128,128]{1,0:T(8,128)S(1)} custom-call(f32[128,128]{1,0:T(8,128)S(1)} %cholesky.584), custom_call_target="Cholesky" | custom-call | tf_op jit(solution)/shard_map/jit(cholesky)/cholesky | solution.py:19
  393.4 9.8 %custom-call.63 = f32[1,128,128]{1,2,0:T(8,128)S(1)} custom-call(f32[1,128,128]{2,1,0:T(8,128)S(1)} %get-tuple-element.41), custom_call_target="InvertDiagBlocksLowerTriangular" | custom-call | tf_op jit(solution)/shard_map/jit(cholesky)/cholesky | solution.py:19
  403.2 1.2 convolution_dynamic-update-slice_fusion
  404.5 2.1 convolution_subtract_fusion.1
  406.6 11.7 %cholesky.468 = f32[128,128]{1,0:T(8,128)S(1)} custom-call(f32[128,128]{1,0:T(8,128)S(1)} %cholesky.589), custom_call_target="Cholesky" | custom-call | tf_op jit(solution)/shard_map/jit(cholesky)/cholesky | solution.py:19
  419.0 0.6 compare_reduce_fusion.5
  419.6 9.8 %custom-call.64 = f32[1,128,128]{1,2,0:T(8,128)S(1)} custom-call(f32[1,128,128]{2,1,0:T(8,128)S(1)} %get-tuple-element.38), custom_call_target="InvertDiagBlocksLowerTriangular" | custom-call | tf_op jit(solution)/shard_map/jit(cholesky)/cholesky | solution.py:19
  429.4 1.2 convolution_dynamic-update-slice_fusion.1
  430.6 2.3 convolution_subtract_fusion.2
  432.9 12.1 %cholesky.487 = f32[128,128]{1,0:T(8,128)S(1)} custom-call(f32[128,128]{1,0:T(8,128)S(1)} %cholesky.594), custom_call_target="Cholesky" | custom-call | tf_op jit(solution)/shard_map/jit(cholesky)/cholesky | solution.py:19
  446.3 9.8 %custom-call.65 = f32[1,128,128]{1,2,0:T(8,128)S(1)} custom-call(f32[1,128,128]{2,1,0:T(8,128)S(1)} %get-tuple-element.35), custom_call_target="InvertDiagBlocksLowerTriangular" | custom-call | tf_op jit(solution)/shard_map/jit(cholesky)/cholesky | solution.py:19
  456.1 1.1 convolution_dynamic-update-slice_fusion.2
  457.2 2.4 convolution_subtract_fusion.3
  459.6 11.7 %cholesky.506 = f32[128,128]{1,0:T(8,128)S(1)} custom-call(f32[128,128]{1,0:T(8,128)S(1)} %cholesky.599), custom_call_target="Cholesky" | custom-call | tf_op jit(solution)/shard_map/jit(cholesky)/cholesky | solution.py:19
  471.3 0.7 select_reduce_fusion.3
  472.0 0.7 compare_reduce_fusion.3
  472.6 9.9 %custom-call.66 = f32[1,128,128]{1,2,0:T(8,128)S(1)} custom-call(f32[1,128,128]{2,1,0:T(8,128)S(1)} %get-tuple-element.32), custom_call_target="InvertDiagBlocksLowerTriangular" | custom-call | tf_op jit(solution)/shard_map/jit(cholesky)/cholesky | solution.py:19
  482.6 1.0 convolution_dynamic-update-slice_fusion.3
  483.6 2.3 convolution_subtract_fusion.4
  485.9 11.7 %cholesky.526 = f32[128,128]{1,0:T(8,128)S(1)} custom-call(f32[128,128]{1,0:T(8,128)S(1)} %cholesky.604), custom_call_target="Cholesky" | custom-call | tf_op jit(solution)/shard_map/jit(cholesky)/cholesky | solution.py:19
  498.9 9.8 %custom-call.67 = f32[1,128,128]{1,2,0:T(8,128)S(1)} custom-call(f32[1,128,128]{2,1,0:T(8,128)S(1)} %get-tuple-element.29), custom_call_target="InvertDiagBlocksLowerTriangular" | custom-call | tf_op jit(solution)/shard_map/jit(cholesky)/cholesky | solution.py:19
  508.7 0.9 convolution_dynamic-update-slice_fusion.4
  509.6 2.0 convolution_subtract_fusion.5
  511.7 11.9 %cholesky.546 = f32[128,128]{1,0:T(8,128)S(1)} custom-call(f32[128,128]{1,0:T(8,128)S(1)} %cholesky.609), custom_call_target="Cholesky" | custom-call | tf_op jit(solution)/shard_map/jit(cholesky)/cholesky | solution.py:19
  523.6 0.7 select_reduce_fusion.1
  524.2 0.7 compare_reduce_fusion.1
  524.9 9.8 %custom-call.68 = f32[1,128,128]{1,2,0:T(8,128)S(1)} custom-call(f32[1,128,128]{2,1,0:T(8,128)S(1)} %get-tuple-element.26), custom_call_target="InvertDiagBlocksLowerTriangular" | custom-call | tf_op jit(solution)/shard_map/jit(cholesky)/cholesky | solution.py:19
  534.7 0.8 convolution_dynamic-update-slice_fusion.5
  535.6 1.8 convolution_subtract_fusion.10
  537.4 11.7 %cholesky.564 = f32[128,128]{1,0:T(8,128)S(1)} custom-call(f32[128,128]{1,0:T(8,128)S(1)} %convolution_subtract_fusion.10), custom_call_target="Cholesky" | custom-call | tf_op jit(solution)/shard_map/jit(cholesky)/cholesky | solution.py:19
  549.1 0.6 select_reduce_fusion
  550.4 0.7 compare_reduce_fusion.6
  556.0 4.8 select_select_fusion
  560.8 22.9 %while.1 = (s32[]{:T(128)}, f32[1024,1024]{1,0:T(8,128)}, s32[8,2]{0,1:T(2,128)S(1)}, f32[8,128,128]{2,1,0:T(8,128)S(1)}, s32[]{:T(128)}) while((s32[]{:T(128)}, f32[1024,1024]{1,0:T(8,128)}, s32[8,2]{0,1:T(2,128)S(1)}, f32[8,128,128]{2,1,0:T(8,128)S(1)}, s32[]{:T(128)}) %tuple.38), condition=%wide.while_cond, body=%wide.while_body.sunk | while | flops 2 | bytes 131181 | solution.py:25
  561.4 2.2 bitcast_dynamic-update-slice_fusion.2
  564.3 2.2 bitcast_dynamic-update-slice_fusion.2
  567.2 2.2 bitcast_dynamic-update-slice_fusion.2
  570.0 2.2 bitcast_dynamic-update-slice_fusion.2
  572.9 2.2 bitcast_dynamic-update-slice_fusion.2
  575.8 2.2 bitcast_dynamic-update-slice_fusion.2
  578.7 2.2 bitcast_dynamic-update-slice_fusion.2
  581.5 2.2 bitcast_dynamic-update-slice_fusion.2
  583.7 78.8 %custom-call.69 = f32[8,128,128]{1,2,0:T(8,128)S(1)} custom-call(f32[8,128,128]{2,1,0:T(8,128)S(1)} %get-tuple-element.12), custom_call_target="InvertDiagBlocksLowerTriangular" | custom-call | tf_op jit(solution)/shard_map/triangular_solve | solution.py:25
  662.8 1.1 convolution_subtract_fusion.9
  664.2 1.3 convolution_subtract_fusion.8
  665.8 1.4 convolution_subtract_fusion.7
  667.5 1.5 convolution_subtract_fusion.12
  669.4 1.7 convolution_subtract_fusion.11
  671.4 1.8 convolution_subtract_fusion.13
  673.6 1.9 convolution_subtract_fusion.6
  675.9 14.7 %fusion.63 = f32[64,4096]{1,0:T(8,128)} fusion(f32[1024,64]{0,1:T(8,128)S(1)} %constant_dynamic-update-slice_fusion.18, f32[1024,4096]{1,0:T(8,128)} %all-gather.3.cloned.1.call-done), kind=kOutput, calls=%fused_computation.159 | convolution fusion | flops 3221225472 | bytes 18087936 | tf_op jit(solution)/shard_map/dot_general | solution.py:29
  (72 shorter events, 12.0 us)
Async XLA Ops:
  6.5 116.6 %all-gather.3.cloned.1.call-start = ((), (), s32[]{:S(2)}) async-start(), calls=%async_computation | async-start | bytes 17825792 | tf_op jit(solution)/shard_map/all_gather | solution.py:10
  7.3 264.4 %all-reduce.3.cloned.1.call-start = ((), (), s32[]{:S(2)}) async-start(), calls=%async_computation.1 | async-start | bytes 524288 | tf_op jit(solution)/shard_map/psum | solution.py:17
  143.6 197.4 %all-gather.5.cloned.1.call-start = ((), (), s32[]{:S(2)}) async-start(), calls=%async_computation.2 | async-start | bytes 4456448 | tf_op jit(solution)/shard_map/all_gather | solution.py:18
  351.0 1.9 copy-start
Sparse Core Ops, SparseCore 0:
  10.1 112.9 all-gather.2
  143.7 127.8 all-reduce.2
  274.8 66.1 all-gather.4
where the time goes:
time: 709 us; the launch traced here: 698 us
  waiting for transfers between devices  314 us (44%)
  other arithmetic  261 us (37%)
  matrix products  71.1 us (10%)
  local copies, waits for them, and re-layouts  32.8 us (5%)
  between operations  19 us (3%)
    another operation x30, other arithmetic, local(): factor = jnp.linalg.cholesky(margin)  172 us
    psum x1, waiting for transfers between devices, local(): summed = lax.psum(partial_value, 'ga')  128 us
    all_gather x1, waiting for transfers between devices, local(): gathered = lax.all_gather(coeffs, 'band', axis=0, tiled=True)  116 us
    another operation x3, other arithmetic, local(): lax.linalg.triangular_solve(factor, selector, left_side=True, lower=True,...  83.6 us
    all_gather x1, waiting for transfers between devices, local(): margin = lax.all_gather(summed, 'band', axis=0, tiled=True)  69.2 us
    another operation x14, matrix products, local(): factor = jnp.linalg.cholesky(margin)  23.1 us
    another operation x24, local copies, waits for them, and re-layouts  22.7 us
    dot_general x1, matrix products, local(): jnp.dot(coeffs, gathered.T, precision=lax.Precision.HIGHEST, preferred_el...  20.5 us
  transfers between devices with their start and end apart: 3, of which 3 were waited for; matrix products, arithmetic and copies ran while one was open for 0% of the time, Pallas kernels for 0%

commit v1 on v0

v1 whole, which is shorter than its diff:
```python
import functools

import jax
import jax.numpy as jnp
from jax import lax
from jax.experimental import pallas as pl
from jax.experimental.pallas import tpu as pltpu
from jax.sharding import PartitionSpec as P

MESH = pl.DeviceIdType.MESH

B = 128
V = 8


def split(x):
    hi = x.astype(jnp.bfloat16)
    return hi, (x - hi.astype(jnp.float32)).astype(jnp.bfloat16)


def dot3(a, b, dims):
    (ca,), (cb,) = dims
    ah, al = a
    bh, bl = b
    left = jnp.concatenate([ah, al, ah], axis=ca)
    right = jnp.concatenate([bh, bh, bl], axis=cb)
    return lax.dot_general(left, right, (dims, ((), ())), preferred_element_type=jnp.float32)


def lane_col(t, c):
    return jnp.broadcast_to(t[:, c : c + 1], (V, B))


def sub_row(t, k):
    return jnp.broadcast_to(t[k : k + 1, :], (V, B))


def factor_inverse(rows):
    n = len(rows)
    sub = lax.broadcasted_iota(jnp.int32, (V, B), 0)
    lane = lax.broadcasted_iota(jnp.int32, (V, B), 1)
    out = []
    for p in range(n):
        c0 = p * V
        in_block = (lane >= c0) & (lane < c0 + V)
        cols = [lane_col(rows[p], c0 + k) for k in range(V)]
        t = jnp.where(in_block, jnp.where(lane - c0 == sub, 1.0, 0.0), rows[p])
        f = jnp.where(lane < c0 + V, t, 0.0)
        pivots = jnp.zeros((V, B), jnp.float32)
        for k in range(V):
            d = sub_row(cols[k], k)
            r = 1.0 / d
            pivots = jnp.where(sub == k, d, pivots)
            here = sub == k
            mult = jnp.where(here, 0.0, cols[k])
            below = jnp.where(sub > k, cols[k], 0.0)
            for j in range(k + 1, V):
                u = sub_row(cols[j], k) * r
                cols[j] = jnp.where(here, u, cols[j] - mult * u)
            u = sub_row(t, k) * r
            t = jnp.where(here, u, t - mult * u)
            if k < V - 1:
                f = f - below * (sub_row(f, k) * r)
        out.append(f * lax.rsqrt(pivots))
        w = [sub_row(t, k) for k in range(V)]
        for q in range(p + 1, n):
            acc = jnp.where(in_block, 0.0, rows[q])
            m = [lane_col(rows[q], c0 + k) * w[k] for k in range(V)]
            while len(m) > 1:
                m = [m[2 * e] + m[2 * e + 1] for e in range(len(m) // 2)]
            rows[q] = acc - m[0]
    return out


def blocks_of(n):
    order, at = [], {}
    for i in range(n):
        for j in range(i, n):
            at[i, j] = len(order)
            order.append((i, j))
    return order, at


def elim_kernel(n, g_ref, c_ref, x_ref, a_ref, z_ref):
    width = c_ref.shape[1]
    order, at = blocks_of(n)
    tiles = B // V
    for i, j in order:
        a_ref[i, :, j * B : (j + 1) * B] = g_ref[at[i, j] * tiles : (at[i, j] + 1) * tiles].reshape(B, B)
    for i in range(n):
        a_ref[i, :, n * B :] = c_ref[i * B : (i + 1) * B, :]

    def step(i, carry):
        here = pl.multiple_of(i * B, B)
        rows = [a_ref[i, q * V : (q + 1) * V, pl.ds(here, B)] for q in range(tiles)]
        for q, z in enumerate(factor_inverse(rows)):
            z_ref[q * V : (q + 1) * V, :] = z
        for k in range(n):

            @pl.when(i == k)
            def _():
                z = split(z_ref[...])
                panel = dot3(z, split(a_ref[k, :, (k + 1) * B :]), ((1,), (0,)))
                x_ref[k * B : (k + 1) * B, :] = panel[:, panel.shape[1] - width :]
                ph, plo = split(panel)
                for j in range(k + 1, n):
                    at_j = (j - k - 1) * B
                    left = (ph[:, at_j : at_j + B], plo[:, at_j : at_j + B])
                    right = (ph[:, at_j:], plo[:, at_j:])
                    a_ref[j, :, j * B :] -= dot3(left, right, ((0,), (0,)))

        return carry

    lax.fori_loop(0, n, step, 0)


def eliminate(g, c):
    rows, width = c.shape
    n = rows // B
    return pl.pallas_call(
        lambda *refs: elim_kernel(n, *refs),
        out_shape=jax.ShapeDtypeStruct((rows, width), jnp.float32),
        in_specs=[pl.BlockSpec(memory_space=pltpu.VMEM)] * 2,
        out_specs=pl.BlockSpec(memory_space=pltpu.VMEM),
        scratch_shapes=[
            pltpu.VMEM((n, B, n * B + width), jnp.float32),
            pltpu.VMEM((B, B), jnp.float32),
        ],
        compiler_params=pltpu.CompilerParams(vmem_limit_bytes=48 << 20),
        name="eliminate",
    )(g, c)


def gram_kernel(scale, c_ref, g_ref):
    rows, depth = c_ref.shape
    n = rows // B
    order, at = blocks_of(n)
    tiles = B // V
    hi, lo = split(c_ref[...])
    for i in range(n):
        left = (hi[i * B : (i + 1) * B], lo[i * B : (i + 1) * B])
        right = (hi[i * B :], lo[i * B :])
        out = dot3(left, right, ((1,), (1,))) * scale
        for j in range(i, n):
            block = out[:, (j - i) * B : (j - i + 1) * B]
            g_ref[at[i, j] * tiles : (at[i, j] + 1) * tiles] = block.reshape(tiles, V, B)


def gram(c, columns_all):
    rows, _ = c.shape
    n = rows // B
    total = n * (n + 1) // 2 * (B // V)
    return pl.pallas_call(
        lambda *refs: gram_kernel(1.0 / columns_all, *refs),
        out_shape=jax.ShapeDtypeStruct((total, V, B), jnp.float32),
        in_specs=[pl.BlockSpec(memory_space=pltpu.VMEM)],
        out_specs=pl.BlockSpec(memory_space=pltpu.VMEM),
        compiler_params=pltpu.CompilerParams(vmem_limit_bytes=48 << 20),
        name="gram",
    )(c)


def exchange_kernel(n, forward, src_ref, dst_ref, send_sem, recv_sem, own_sem):
    me = lax.axis_index("band")
    barrier = pltpu.get_barrier_semaphore()
    rows, cols = (src_ref if forward else dst_ref).shape
    width = cols // n

    def part(ref, split_columns, index):
        if split_columns:
            return ref.at[:, pl.ds(pl.multiple_of(index * width, width), width)]
        return ref.at[pl.ds(pl.multiple_of(index * rows, rows), rows), :]

    def greet(s, carry):
        pl.semaphore_signal(
            barrier, inc=1, device_id={"band": lax.rem(me + s, n)}, device_id_type=MESH
        )
        return carry

    lax.fori_loop(1, n, greet, 0)
    own = pltpu.make_async_copy(part(src_ref, forward, me), part(dst_ref, not forward, me), own_sem)
    own.start()
    pl.semaphore_wait(barrier, n - 1)

    def copy(s):
        peer = lax.rem(me + s, n)
        return pltpu.make_async_remote_copy(
            src_ref=part(src_ref, forward, peer),
            dst_ref=part(dst_ref, not forward, me),
            send_sem=send_sem.at[s],
            recv_sem=recv_sem.at[s],
            device_id={"band": peer},
            device_id_type=MESH,
        )

    def start(s, carry):
        copy(s).start()
        return carry

    def wait(s, carry):
        peer = lax.rem(me - s + n, n)
        got = pltpu.make_async_remote_copy(
            src_ref=part(src_ref, forward, lax.rem(me + s, n)),
            dst_ref=part(dst_ref, not forward, peer),
            send_sem=send_sem.at[s],
            recv_sem=recv_sem.at[s],
            device_id={"band": lax.rem(me + s, n)},
            device_id_type=MESH,
        )
        got.wait()
        return carry

    lax.fori_loop(1, n, start, 0)
    own.wait()
    lax.fori_loop(1, n, wait, 0)


def exchange(x, n, forward):
    rows, cols = x.shape
    shape = (rows * n, cols // n) if forward else (rows // n, cols * n)
    return pl.pallas_call(
        functools.partial(exchange_kernel, n, forward),
        out_shape=jax.ShapeDtypeStruct(shape, x.dtype),
        in_specs=[pl.BlockSpec(memory_space=pl.ANY)],
        out_specs=pl.BlockSpec(memory_space=pl.ANY),
        scratch_shapes=[
            pltpu.SemaphoreType.DMA((n,)),
            pltpu.SemaphoreType.DMA((n,)),
            pltpu.SemaphoreType.DMA,
        ],
        compiler_params=pltpu.CompilerParams(
            collective_id=0 if forward else 1, has_side_effects=True
        ),
        name="exchange" if forward else "exchange_back",
    )(x)


CORES, YS, XS, ZS = 2, 4, 4, 8
HALF = 288
FIRST = HALF // 4
SECOND = FIRST // 4
Z_USED = 6
THIRD = SECOND // Z_USED


def coordinates():
    band, ga = lax.axis_index("band"), lax.axis_index("ga")
    core, y = lax.rem(band, CORES), lax.rem(band // CORES, YS)
    x = (band // (CORES * YS)) * 2 + lax.rem(ga, 2)
    return core, x, y, ga // 2


def device(core, x, y, z):
    return {"band": ((x // 2) * YS + y) * CORES + core, "ga": z * 2 + lax.rem(x, 2)}


def sum_kernel(p_ref, o_ref, acc1, acc2, acc3, got0, got1, got2, got3, send, recv):
    core, x, y, z = coordinates()
    first_is_y = core == 0
    a = jnp.where(first_is_y, y, x)
    b = jnp.where(first_is_y, x, y)

    def first_peer(s):
        to = lax.rem(a + s, 4)
        return to, device(core, jnp.where(first_is_y, x, to), jnp.where(first_is_y, to, y), z)

    def second_peer(s):
        to = lax.rem(b + s, 4)
        return to, device(core, jnp.where(first_is_y, to, x), jnp.where(first_is_y, y, to), z)

    def z_peer(s):
        to = lax.rem(z + s, ZS)
        return to, device(core, x, y, to)

    partner = device(1 - core, x, y, z)

    barrier = pltpu.get_barrier_semaphore()
    peers = [partner]
    peers += [first_peer(s)[1] for s in range(1, 4)]
    peers += [second_peer(s)[1] for s in range(1, 4)]
    peers += [z_peer(s)[1] for s in range(1, ZS)]
    for peer in peers:
        pl.semaphore_signal(barrier, inc=1, device_id=peer, device_id_type=MESH)
    pl.semaphore_wait(barrier, len(peers))

    def copy(src, dst, index, peer):
        return pltpu.make_async_remote_copy(
            src_ref=src,
            dst_ref=dst,
            send_sem=send.at[index],
            recv_sem=recv.at[index],
            device_id=peer,
            device_id_type=MESH,
        )

    mine = core * HALF
    c = copy(p_ref.at[pl.ds((1 - core) * HALF, HALF)], got0, 0, partner)
    c.start()
    c.wait()

    def add0(t, carry):
        at = pl.ds(t * 8, 8)
        acc1[at] = p_ref[pl.ds(mine + t * 8, 8)] + got0[at]
        return carry

    lax.fori_loop(0, HALF // 8, add0, 0)

    started = []
    for s in range(1, 4):
        to, peer = first_peer(s)
        c = copy(acc1.at[pl.ds(to * FIRST, FIRST)], got1.at[s - 1], s, peer)
        c.start()
        started.append(c)
    for c in started:
        c.wait()

    def add1(t, carry):
        at = pl.ds(t * 8, 8)
        acc2[at] = (acc1[pl.ds(a * FIRST + t * 8, 8)] + got1[0, at]) + (got1[1, at] + got1[2, at])
        return carry

    lax.fori_loop(0, FIRST // 8, add1, 0)
    started = []
    for s in range(1, 4):
        to, peer = second_peer(s)
        c = copy(acc2.at[pl.ds(to * SECOND, SECOND)], got2.at[s - 1], 3 + s, peer)
        c.start()
        started.append(c)
    for c in started:
        c.wait()
    at = pl.ds(b * SECOND, SECOND)
    acc3[...] = (acc2[at] + got2[0]) + (got2[1] + got2[2])

    for s in range(1, ZS):
        to, peer = z_peer(s)

        @pl.when(to < Z_USED)
        def _():
            copy(acc3.at[pl.ds(to * THIRD, THIRD)], got3.at[s - 1], 6 + s, peer).start()

    base2 = mine + a * FIRST
    base3 = base2 + b * SECOND
    own = base3 + z * THIRD

    @pl.when(z < Z_USED)
    def _():
        for s in range(1, ZS):
            copy(acc3.at[pl.ds(0, THIRD)], got3.at[s - 1], 6 + s, partner).wait_recv()
        total = acc3[pl.ds(z * THIRD, THIRD)]
        for s in range(1, ZS):
            total = total + got3[s - 1]
        o_ref[pl.ds(own, THIRD)] = total

    for s in range(1, ZS):
        to, peer = z_peer(s)

        @pl.when(to < Z_USED)
        def _():
            copy(acc3.at[pl.ds(0, THIRD)], got3.at[s - 1], 6 + s, peer).wait_send()

    @pl.when(z < Z_USED)
    def _():
        for s in range(1, ZS):
            to, peer = z_peer(s)
            copy(o_ref.at[pl.ds(own, THIRD)], o_ref.at[pl.ds(own, THIRD)], 13 + s, peer).start()

    for s in range(1, ZS):
        sender = lax.rem(z + ZS - s, ZS)

        @pl.when(sender < Z_USED)
        def _():
            chunk = o_ref.at[pl.ds(base3 + sender * THIRD, THIRD)]
            copy(chunk, chunk, 13 + s, partner).wait_recv()

    @pl.when(z < Z_USED)
    def _():
        for s in range(1, ZS):
            to, peer = z_peer(s)
            copy(o_ref.at[pl.ds(own, THIRD)], o_ref.at[pl.ds(own, THIRD)], 13 + s, peer).wait_send()

    def spread(base, at, size, index, peers_of, count):
        chunk = o_ref.at[pl.ds(base + at * size, size)]
        for s in range(1, count):
            copy(chunk, chunk, index + s, peers_of(s)[1]).start()
        for s in range(1, count):
            sender = lax.rem(at + count - s, count)
            got = o_ref.at[pl.ds(base + sender * size, size)]
            copy(chunk, got, index + s, peers_of(s)[1]).wait()

    spread(base2, b, SECOND, 20, second_peer, 4)
    spread(mine, a, FIRST, 23, first_peer, 4)
    spread(0, core, HALF, 26, lambda s: (1 - core, partner), 2)


def sum_tiles(p):
    vmem = pl.BlockSpec(memory_space=pltpu.VMEM)
    tiles = lambda *shape: pltpu.VMEM((*shape, V, B), jnp.float32)
    return pl.pallas_call(
        sum_kernel,
        out_shape=jax.ShapeDtypeStruct(p.shape, p.dtype),
        in_specs=[vmem],
        out_specs=vmem,
        scratch_shapes=[
            tiles(HALF),
            tiles(FIRST),
            tiles(SECOND),
            tiles(HALF),
            tiles(3, FIRST),
            tiles(3, SECOND),
            tiles(7, THIRD),
            pltpu.SemaphoreType.DMA((28,)),
            pltpu.SemaphoreType.DMA((28,)),
        ],
        compiler_params=pltpu.CompilerParams(
            collective_id=2, has_side_effects=True, vmem_limit_bytes=48 << 20
        ),
        name="sum_tiles",
    )(p)


def local(coeffs):
    bands = lax.axis_size("band")
    columns_all = coeffs.shape[1] * lax.axis_size("ga")
    held = exchange(coeffs, bands, True)
    margin = sum_tiles(gram(held, columns_all))
    return exchange(eliminate(margin, held), bands, False)


def solution(mesh):
    return jax.shard_map(
        local,
        mesh=mesh,
        in_specs=(P("band", "ga"),),
        out_specs=P("band", "ga"),
        check_vma=False,
    )
```

time: 709 us -> 147 us (0.21); the launches traced: 698 us -> 146 us
  waiting for transfers between devices: 314 us -> 0 us
  other arithmetic: 261 us -> 0 us
  Pallas kernels: 0 us -> 141 us
  matrix products: 71.1 us -> 0 us
  local copies, waits for them, and re-layouts: 32.8 us -> 4.46 us
  between operations: 19 us -> 0.07 us
    another operation x33 -> x0, other arithmetic: 256 us -> none  [the longest x30 172 us: local(): factor = jnp.linalg.cholesky(margin)]
    all_gather x2 -> x0, waiting for transfers between devices: 185 us -> none  [the longest x1 116 us: local(): gathered = lax.all_gather(coeffs, 'band', axis=0, tiled=True)]
    pallas_call x0 -> x5, Pallas kernels: none -> 141 us  [the longest x1 51.8 us: sum_tiles(): pl.pallas_call(sum_kernel, out_shape=jax.ShapeDtypeStruct(p.shape, p.dtyp...]
    psum x1 -> x0, waiting for transfers between devices: 128 us -> none  [local(): summed = lax.psum(partial_value, 'ga')]
    another operation x29 -> x0, matrix products: 36 us -> none  [the longest x14 23.1 us: local(): factor = jnp.linalg.cholesky(margin)]
    dot_general x2 -> x0, matrix products: 35.1 us -> none  [the longest x1 20.5 us: local(): jnp.dot(coeffs, gathered.T, precision=lax.Precision.HIGHEST, preferred_el...]
    another operation x37 -> x0, local copies, waits for them, and re-layouts: 25.3 us -> none
  transfers between devices with their start and end apart: 3 -> 0, of which waited for: 3 -> 0; matrix products, arithmetic and copies ran while one was open for 0% -> 0% of each run, Pallas kernels for 0% -> 0%
where the time goes in v1:
time: 147 us; the launch traced here: 146 us
  Pallas kernels  141 us (96%)
  local copies, waits for them, and re-layouts  4.46 us (3%)
    pallas_call x1, Pallas kernels, sum_tiles(): pl.pallas_call(sum_kernel, out_shape=jax.ShapeDtypeStruct(p.shape, p.dtyp...  51.8 us
    pallas_call x2, Pallas kernels, exchange(): pl.pallas_call(functools.partial(exchange_kernel, n, forward), out_shape=...  45.2 us
    pallas_call x1, Pallas kernels, eliminate(): pl.pallas_call(lambda *refs: elim_kernel(n, *refs), out_shape=jax.ShapeDt...  42.1 us
    unnamed x7, local copies, waits for them, and re-layouts  4.46 us

profile of v1, /device:TPU:29, one launch (start us, length us, event | category | flops | bytes accessed | tf_op | source)
XLA Modules:
  0.0 145.8 jit_solution(16443921509766998614)
XLA Ops:
  0.0 21.5 %exchange.1.refs_0_.refs_1_ = f32[1024,256]{1,0:T(8,128)} custom-call(f32[64,4096]{1,0:T(8,128)} %src_ref.1), custom_call_target="tpu_custom_call" | custom-call | tf_op jit(solution)/shard_map/exchange/pallas_call | solution.py:221
  21.5 0.0 copy-start
  21.5 1.2 copy-done
  22.7 2.2 %gram.1.p_ref = f32[576,8,128]{2,1,0:T(8,128)S(1)} custom-call(f32[1024,256]{1,0:T(8,128)S(1)} %copy-done), custom_call_target="tpu_custom_call" | custom-call | tf_op jit(solution)/shard_map/gram/pallas_call | solution.py:153
  24.9 0.0 copy-start.1
  24.9 51.8 %sum_tiles.1.refs_0_ = f32[576,8,128]{2,1,0:T(8,128)S(1)} custom-call(f32[576,8,128]{2,1,0:T(8,128)S(1)} %gram.1.p_ref), custom_call_target="tpu_custom_call" | custom-call | tf_op jit(solution)/shard_map/sum_tiles/pallas_call | solution.py:398
  76.8 0.0 copy-done.1
  76.8 42.1 %eliminate.1.src_ref = f32[1024,256]{1,0:T(8,128)S(1)} custom-call(f32[576,8,128]{2,1,0:T(8,128)S(1)} %sum_tiles.1.refs_0_, f32[1024,256]{1,0:T(8,128)S(1)} %copy-done.1), custom_call_target="tpu_custom_call" | custom-call | tf_op jit(solution)/shard_map/eliminate/pallas_call | solution.py:120
  118.9 0.0 copy-start.2
  118.9 1.0 copy-done.2
  119.9 23.7 %exchange_back.1 = f32[64,4096]{1,0:T(8,128)} custom-call(f32[1024,256]{1,0:T(8,128)} %copy-done.2), custom_call_target="tpu_custom_call" | custom-call | tf_op jit(solution)/shard_map/exchange_back/pallas_call | solution.py:221
  143.5 2.3 %copy.3 = f32[64,4096]{1,0:T(8,128)} copy(f32[64,4096]{1,0:T(8,128)} %exchange_back.1) | data formatting | bytes 2097152
Async XLA Ops:
  21.5 1.2 copy-start
  24.9 51.8 %copy-start.1 = (f32[1024,256]{1,0:T(8,128)S(1)}, f32[1024,256]{1,0:T(8,128)}, u32[]{:S(2)}) copy-start(f32[1024,256]{1,0:T(8,128)} %exchange.1.refs_0_.refs_1_) | copy-start | bytes 3145732
  118.9 1.0 copy-start.2

commit v2 on v1

--- a/solution.py
+++ b/solution.py
@@ -28,47 +28,84 @@
 
 
 def lane_col(t, c):
-    return jnp.broadcast_to(t[:, c : c + 1], (V, B))
+    return jnp.take_along_axis(t, jnp.full((V, B), c, jnp.int32), axis=1)
 
 
 def sub_row(t, k):
     return jnp.broadcast_to(t[k : k + 1, :], (V, B))
 
 
+def tree(m):
+    while len(m) > 1:
+        m = [m[e] + m[e + 1] if e + 1 < len(m) else m[e] for e in range(0, len(m), 2)]
+    return m[0]
+
+
 def factor_inverse(rows):
     n = len(rows)
+    rows = list(rows)
     sub = lax.broadcasted_iota(jnp.int32, (V, B), 0)
     lane = lax.broadcasted_iota(jnp.int32, (V, B), 1)
     out = []
+    cols = [lane_col(rows[0], k) for k in range(V)]
     for p in range(n):
         c0 = p * V
+        last = p == n - 1
         in_block = (lane >= c0) & (lane < c0 + V)
-        cols = [lane_col(rows[p], c0 + k) for k in range(V)]
         t = jnp.where(in_block, jnp.where(lane - c0 == sub, 1.0, 0.0), rows[p])
         f = jnp.where(lane < c0 + V, t, 0.0)
-        pivots = jnp.zeros((V, B), jnp.float32)
-        for k in range(V):
-            d = sub_row(cols[k], k)
-            r = 1.0 / d
-            pivots = jnp.where(sub == k, d, pivots)
-            here = sub == k
-            mult = jnp.where(here, 0.0, cols[k])
-            below = jnp.where(sub > k, cols[k], 0.0)
-            for j in range(k + 1, V):
-                u = sub_row(cols[j], k) * r
-                cols[j] = jnp.where(here, u, cols[j] - mult * u)
-            u = sub_row(t, k) * r
-            t = jnp.where(here, u, t - mult * u)
-            if k < V - 1:
-                f = f - below * (sub_row(f, k) * r)
-        out.append(f * lax.rsqrt(pivots))
+        pivots = None
+        below_m = {q: [lane_col(rows[q], c0 + k) for k in range(V)] for q in range(p + 1, n)}
+        if not last:
+            a = list(below_m[p + 1])
+            ahead = [lane_col(rows[p + 1], c0 + V + k) for k in range(V)]
+        for k in range(0, V, 2):
+            h1, h2 = sub == k, sub == k + 1
+            here = h1 | h2
+            d11, d12, d22 = sub_row(cols[k], k), sub_row(cols[k + 1], k), sub_row(cols[k + 1], k + 1)
+            det = d11 * d22 - d12 * d12
+            r = 1.0 / det
+            m1, m2 = jnp.where(here, 0.0, cols[k]), jnp.where(here, 0.0, cols[k + 1])
+
+            def solve(col):
+                v1, v2 = sub_row(col, k), sub_row(col, k + 1)
+                return (d22 * v1 - d12 * v2) * r, (d11 * v2 - d12 * v1) * r
+
+            def eliminate(col):
+                u1, u2 = solve(col)
+                return jnp.where(h1, u1, jnp.where(h2, u2, col - (m1 * u1 + m2 * u2))), u1, u2
+
+            for j in range(k + 2, V):
+                cols[j], u1, u2 = eliminate(cols[j])
+                if not last:
+                    a[j] = a[j] - (a[k] * u1 + a[k + 1] * u2)
+            if not last:
+                s1 = (d22 * a[k] - d12 * a[k + 1]) * r
+                s2 = (d11 * a[k + 1] - d12 * a[k]) * r
+                for j in range(V):
+                    ahead[j] = ahead[j] - (s1 * sub_row(a[k], j) + s2 * sub_row(a[k + 1], j))
+            q = 1.0 / d11
+            ratio = d12 * q
+            f1 = sub_row(f, k)
+            f2 = sub_row(f, k + 1) - ratio * f1
+            g2 = d11 * r
+            g1 = q
+            below = sub > k + 1
+            b1 = jnp.where(below, cols[k], 0.0)
+            b2 = jnp.where(below, cols[k + 1], 0.0)
+            l2 = b2 - b1 * ratio
+            f = jnp.where(h2, f2, f - b1 * (f1 * g1) - l2 * (f2 * g2))
+            t, _, _ = eliminate(t)
+            scale = jnp.where(h1, g1, g2)
+            pivots = scale if pivots is None else jnp.where(here, scale, pivots)
+        out.append(f * jnp.sqrt(pivots))
+        if last:
+            break
+        cols = ahead
         w = [sub_row(t, k) for k in range(V)]
         for q in range(p + 1, n):
             acc = jnp.where(in_block, 0.0, rows[q])
-            m = [lane_col(rows[q], c0 + k) * w[k] for k in range(V)]
-            while len(m) > 1:
-                m = [m[2 * e] + m[2 * e + 1] for e in range(len(m) // 2)]
-            rows[q] = acc - m[0]
+            rows[q] = acc - tree([below_m[q][k] * w[k] for k in range(V)])
     return out
 
 
@@ -81,14 +118,62 @@
     return order, at
 
 
-def elim_kernel(n, g_ref, c_ref, x_ref, a_ref, z_ref):
+def elim_kernel(n, g_ref, c_ref, out_ref, a_ref, z_ref, x_ref, send_sem, recv_sem, own_sem):
     width = c_ref.shape[1]
+    rows_each = out_ref.shape[0]
+    bands = n * B // rows_each
+    per_panel = B // rows_each
+    me = lax.axis_index("band")
+    barrier = pltpu.get_barrier_semaphore()
+
+    def greet(s, carry):
+        pl.semaphore_signal(
+            barrier, inc=1, device_id={"band": lax.rem(me + s, bands)}, device_id_type=MESH
+        )
+        return carry
+
+    lax.fori_loop(1, bands, greet, 0)
     order, at = blocks_of(n)
     tiles = B // V
+
+    sub = lax.broadcasted_iota(jnp.int32, (V, B), 0)
+    lane = lax.broadcasted_iota(jnp.int32, (V, B), 1)
+    lane_scale, row_scale = [], []
+    for i in range(n):
+        on_diagonal = [
+            jnp.where(lane == q * V + sub, g_ref[at[i, i] * tiles + q], 0.0) for q in range(tiles)
+        ]
+        diagonal = jnp.sum(tree(on_diagonal), axis=0, keepdims=True)
+        scale = jnp.broadcast_to(lax.rsqrt(diagonal), (V, B))
+        lane_scale.append(scale)
+        row_scale.append([jnp.take_along_axis(scale, q * V + sub, axis=1) for q in range(tiles)])
     for i, j in order:
-        a_ref[i, :, j * B : (j + 1) * B] = g_ref[at[i, j] * tiles : (at[i, j] + 1) * tiles].reshape(B, B)
+        for q in range(tiles):
+            a_ref[i, q * V : (q + 1) * V, j * B : (j + 1) * B] = (
+                g_ref[at[i, j] * tiles + q] * row_scale[i][q] * lane_scale[j]
+            )
     for i in range(n):
-        a_ref[i, :, n * B :] = c_ref[i * B : (i + 1) * B, :]
+        for q in range(tiles):
+            for h in range(width // B):
+                a_ref[i, q * V : (q + 1) * V, (n + h) * B : (n + h + 1) * B] = (
+                    c_ref[i * B + q * V : i * B + (q + 1) * V, h * B : (h + 1) * B] * row_scale[i][q]
+                )
+
+    def remote(peer, sender):
+        return pltpu.make_async_remote_copy(
+            src_ref=x_ref.at[pl.ds(peer * rows_each, rows_each), :],
+            dst_ref=out_ref.at[:, pl.ds(pl.multiple_of(sender * width, width), width)],
+            send_sem=send_sem.at[peer],
+            recv_sem=recv_sem.at[sender],
+            device_id={"band": peer},
+            device_id_type=MESH,
+        )
+
+    own = pltpu.make_async_copy(
+        x_ref.at[pl.ds(me * rows_each, rows_each), :],
+        out_ref.at[:, pl.ds(pl.multiple_of(me * width, width), width)],
+        own_sem,
+    )
 
     def step(i, carry):
         here = pl.multiple_of(i * B, B)
@@ -102,6 +187,18 @@
                 z = split(z_ref[...])
                 panel = dot3(z, split(a_ref[k, :, (k + 1) * B :]), ((1,), (0,)))
                 x_ref[k * B : (k + 1) * B, :] = panel[:, panel.shape[1] - width :]
+                if k == 0:
+                    pl.semaphore_wait(barrier, bands - 1)
+                for peer in range(k * per_panel, (k + 1) * per_panel):
+
+                    @pl.when(peer != me)
+                    def _():
+                        remote(peer, me).start()
+
+                    @pl.when(peer == me)
+                    def _():
+                        own.start()
+
                 ph, plo = split(panel)
                 for j in range(k + 1, n):
                     at_j = (j - k - 1) * B
@@ -112,21 +209,34 @@
         return carry
 
     lax.fori_loop(0, n, step, 0)
-
-
-def eliminate(g, c):
+    own.wait()
+    for other in range(bands):
+
+        @pl.when(other != me)
+        def _():
+            remote(other, me).wait_send()
+            remote(other, other).wait_recv()
+
+
+def eliminate(g, c, bands):
     rows, width = c.shape
     n = rows // B
     return pl.pallas_call(
-        lambda *refs: elim_kernel(n, *refs),
-        out_shape=jax.ShapeDtypeStruct((rows, width), jnp.float32),
+        functools.partial(elim_kernel, n),
+        out_shape=jax.ShapeDtypeStruct((rows // bands, width * bands), jnp.float32),
         in_specs=[pl.BlockSpec(memory_space=pltpu.VMEM)] * 2,
         out_specs=pl.BlockSpec(memory_space=pltpu.VMEM),
         scratch_shapes=[
             pltpu.VMEM((n, B, n * B + width), jnp.float32),
             pltpu.VMEM((B, B), jnp.float32),
+            pltpu.VMEM((rows, width), jnp.float32),
+            pltpu.SemaphoreType.DMA((bands,)),
+            pltpu.SemaphoreType.DMA((bands,)),
+            pltpu.SemaphoreType.DMA,
         ],
-        compiler_params=pltpu.CompilerParams(vmem_limit_bytes=48 << 20),
+        compiler_params=pltpu.CompilerParams(
+            collective_id=1, has_side_effects=True, vmem_limit_bytes=48 << 20
+        ),
         name="eliminate",
     )(g, c)
 
@@ -423,7 +533,7 @@
     columns_all = coeffs.shape[1] * lax.axis_size("ga")
     held = exchange(coeffs, bands, True)
     margin = sum_tiles(gram(held, columns_all))
-    return exchange(eliminate(margin, held), bands, False)
+    return eliminate(margin, held, bands)
 
 
 def solution(mesh):

time: 147 us -> 121 us (0.82)
  Pallas kernels: 141 us -> 118 us
  local copies, waits for them, and re-layouts: 4.46 us -> 2.19 us
    pallas_call x2 -> x1, Pallas kernels: 45.2 us -> 21.5 us  [exchange(): pl.pallas_call(functools.partial(exchange_kernel, n, forward), out_shape=...]
    unnamed x7 -> x5, local copies, waits for them, and re-layouts: 4.46 us -> 2.19 us
where the time goes in v2:
time: 121 us; the launch traced here: 120 us
  Pallas kernels  118 us (98%)
  local copies, waits for them, and re-layouts  2.19 us (2%)
    pallas_call x1, Pallas kernels, sum_tiles(): pl.pallas_call(sum_kernel, out_shape=jax.ShapeDtypeStruct(p.shape, p.dtyp...  51.8 us
    pallas_call x1, Pallas kernels, eliminate(): pl.pallas_call(functools.partial(elim_kernel, n), out_shape=jax.ShapeDtyp...  42.2 us
    pallas_call x1, Pallas kernels, exchange(): pl.pallas_call(functools.partial(exchange_kernel, n, forward), out_shape=...  21.5 us

profile of v2, /device:TPU:29, one launch (start us, length us, event | category | flops | bytes accessed | tf_op | source)
XLA Modules:
  0.0 119.9 jit_solution(1922176979506441336)
XLA Ops:
  0.0 21.5 %exchange.1.refs_0_.c_ref = f32[1024,256]{1,0:T(8,128)} custom-call(f32[64,4096]{1,0:T(8,128)} %src_ref.1), custom_call_target="tpu_custom_call" | custom-call | tf_op jit(solution)/shard_map/exchange/pallas_call | solution.py:331
  21.5 0.0 copy-start
  21.5 1.2 %copy-done = f32[1024,256]{1,0:T(8,128)S(1)} copy-done((f32[1024,256]{1,0:T(8,128)S(1)}, f32[1024,256]{1,0:T(8,128)}, u32[]{:S(2)}) %copy-start) | copy-done | bytes 1048600
  22.7 2.2 %gram.1.p_ref = f32[576,8,128]{2,1,0:T(8,128)S(1)} custom-call(f32[1024,256]{1,0:T(8,128)S(1)} %copy-done), custom_call_target="tpu_custom_call" | custom-call | tf_op jit(solution)/shard_map/gram/pallas_call | solution.py:263
  24.9 0.0 copy-start.1
  24.9 51.8 %sum_tiles.1.g_ref = f32[576,8,128]{2,1,0:T(8,128)S(1)} custom-call(f32[576,8,128]{2,1,0:T(8,128)S(1)} %gram.1.p_ref), custom_call_target="tpu_custom_call" | custom-call | tf_op jit(solution)/shard_map/sum_tiles/pallas_call | solution.py:508
  76.8 0.0 copy-done.1
  76.8 42.2 %eliminate.1 = f32[64,4096]{1,0:T(8,128)S(1)} custom-call(f32[576,8,128]{2,1,0:T(8,128)S(1)} %sum_tiles.1.g_ref, f32[1024,256]{1,0:T(8,128)S(1)} %copy-done.1), custom_call_target="tpu_custom_call" | custom-call | tf_op jit(solution)/shard_map/eliminate/pallas_call | solution.py:224
  119.0 1.0 copy.3
Async XLA Ops:
  21.5 1.2 %copy-start = (f32[1024,256]{1,0:T(8,128)S(1)}, f32[1024,256]{1,0:T(8,128)}, u32[]{:S(2)}) copy-start(f32[1024,256]{1,0:T(8,128)} %exchange.1.refs_0_.c_ref) | copy-start | bytes 3145732
  24.9 51.8 %copy-start.1 = (f32[1024,256]{1,0:T(8,128)S(1)}, f32[1024,256]{1,0:T(8,128)}, u32[]{:S(2)}) copy-start(f32[1024,256]{1,0:T(8,128)} %exchange.1.refs_0_.c_ref) | copy-start | bytes 3145732

commit v3 on v0

v3 whole, which is shorter than its diff:
```python
import functools

import jax
import jax.numpy as jnp
from jax import lax
from jax.experimental import pallas as pl
from jax.experimental.pallas import tpu as pltpu
from jax.sharding import PartitionSpec as P

MESH = pl.DeviceIdType.MESH

B = 128
V = 8


def split(x):
    hi = x.astype(jnp.bfloat16)
    return hi, (x - hi.astype(jnp.float32)).astype(jnp.bfloat16)


def dot3(a, b, dims):
    (ca,), (cb,) = dims
    ah, al = a
    bh, bl = b
    left = jnp.concatenate([ah, al, ah], axis=ca)
    right = jnp.concatenate([bh, bh, bl], axis=cb)
    return lax.dot_general(left, right, (dims, ((), ())), preferred_element_type=jnp.float32)


def lane_col(t, c):
    return jnp.take_along_axis(t, jnp.full((V, B), c, jnp.int32), axis=1)


def sub_row(t, k):
    return jnp.broadcast_to(t[k : k + 1, :], (V, B))


def tree(m):
    while len(m) > 1:
        m = [m[e] + m[e + 1] if e + 1 < len(m) else m[e] for e in range(0, len(m), 2)]
    return m[0]


def factor_inverse(rows):
    n = len(rows)
    rows = list(rows)
    sub = lax.broadcasted_iota(jnp.int32, (V, B), 0)
    lane = lax.broadcasted_iota(jnp.int32, (V, B), 1)
    out = []
    cols = [lane_col(rows[0], k) for k in range(V)]
    for p in range(n):
        c0 = p * V
        last = p == n - 1
        in_block = (lane >= c0) & (lane < c0 + V)
        t = jnp.where(in_block, jnp.where(lane - c0 == sub, 1.0, 0.0), rows[p])
        f = jnp.where(lane < c0 + V, t, 0.0)
        pivots = None
        below_m = {q: [lane_col(rows[q], c0 + k) for k in range(V)] for q in range(p + 1, n)}
        if not last:
            a = list(below_m[p + 1])
            ahead = [lane_col(rows[p + 1], c0 + V + k) for k in range(V)]
        for k in range(0, V, 2):
            h1, h2 = sub == k, sub == k + 1
            here = h1 | h2
            d11, d12, d22 = sub_row(cols[k], k), sub_row(cols[k + 1], k), sub_row(cols[k + 1], k + 1)
            det = d11 * d22 - d12 * d12
            r = 1.0 / det
            m1, m2 = jnp.where(here, 0.0, cols[k]), jnp.where(here, 0.0, cols[k + 1])

            def solve(col):
                v1, v2 = sub_row(col, k), sub_row(col, k + 1)
                return (d22 * v1 - d12 * v2) * r, (d11 * v2 - d12 * v1) * r

            def eliminate(col):
                u1, u2 = solve(col)
                return jnp.where(h1, u1, jnp.where(h2, u2, col - (m1 * u1 + m2 * u2))), u1, u2

            for j in range(k + 2, V):
                cols[j], u1, u2 = eliminate(cols[j])
                if not last:
                    a[j] = a[j] - (a[k] * u1 + a[k + 1] * u2)
            if not last:
                s1 = (d22 * a[k] - d12 * a[k + 1]) * r
                s2 = (d11 * a[k + 1] - d12 * a[k]) * r
                for j in range(V):
                    ahead[j] = ahead[j] - (s1 * sub_row(a[k], j) + s2 * sub_row(a[k + 1], j))
            q = 1.0 / d11
            ratio = d12 * q
            f1 = sub_row(f, k)
            f2 = sub_row(f, k + 1) - ratio * f1
            g2 = d11 * r
            g1 = q
            below = sub > k + 1
            b1 = jnp.where(below, cols[k], 0.0)
            b2 = jnp.where(below, cols[k + 1], 0.0)
            l2 = b2 - b1 * ratio
            f = jnp.where(h2, f2, f - b1 * (f1 * g1) - l2 * (f2 * g2))
            t, _, _ = eliminate(t)
            scale = jnp.where(h1, g1, g2)
            pivots = scale if pivots is None else jnp.where(here, scale, pivots)
        out.append(f * jnp.sqrt(pivots))
        if last:
            break
        cols = ahead
        w = [sub_row(t, k) for k in range(V)]
        for q in range(p + 1, n):
            acc = jnp.where(in_block, 0.0, rows[q])
            rows[q] = acc - tree([below_m[q][k] * w[k] for k in range(V)])
    return out


def grouped_blocks(n):
    early = [(i, j) for i in range(2) for j in range(i, n)] + [(2, 2)]
    late = [(i, j) for i in range(2, n) for j in range(i, n) if (i, j) not in early]
    return early, late


def gram_kernel(n, scale, own_ref, other_ref, p_ref):
    core = lax.rem(lax.axis_index("band"), CORES)
    tiles = B // V
    own, other = split(own_ref[...]), split(other_ref[...])
    hi, lo = (jnp.concatenate([o, t], axis=1) for o, t in zip(own, other))
    for c in range(CORES):

        @pl.when(core == c)
        def _():
            mine = []
            for group in grouped_blocks(n):
                half = len(group) // CORES
                mine += group[c * half : (c + 1) * half]
            for i in sorted({i for i, _ in mine}):
                wanted = [j for k, j in mine if k == i]
                first, end = min(wanted), max(wanted) + 1
                left = (hi[i * B : (i + 1) * B], lo[i * B : (i + 1) * B])
                right = (hi[first * B : end * B], lo[first * B : end * B])
                out = dot3(left, right, ((1,), (1,))) * scale
                for j in wanted:
                    at = mine.index((i, j)) * tiles
                    p_ref[at : at + tiles] = out[:, (j - first) * B : (j - first + 1) * B].reshape(tiles, V, B)


def gram(own, other, columns_all):
    n = own.shape[0] // B
    early, late = grouped_blocks(n)
    vmem = pl.BlockSpec(memory_space=pltpu.VMEM)
    return pl.pallas_call(
        functools.partial(gram_kernel, n, 1.0 / columns_all),
        out_shape=jax.ShapeDtypeStruct(((len(early) + len(late)) // CORES * (B // V), V, B), jnp.float32),
        in_specs=[vmem, vmem],
        out_specs=vmem,
        compiler_params=pltpu.CompilerParams(vmem_limit_bytes=48 << 20),
        name="gram",
    )(own, other)


def exchange_kernel(n, src_ref, own_ref, other_ref, send_sem, recv_sem, pass_send, pass_recv, own_sem):
    me = lax.axis_index("band")
    core = lax.rem(me, CORES)
    partner = {"band": me + 1 - 2 * core}
    barrier = pltpu.get_barrier_semaphore()
    rows, cols = src_ref.shape
    width = cols // n

    def columns(index):
        return src_ref.at[:, pl.ds(pl.multiple_of(index * width, width), width)]

    def band(ref, index):
        return ref.at[pl.ds(pl.multiple_of(index * rows, rows), rows), :]

    def greet(s, carry):
        pl.semaphore_signal(
            barrier, inc=1, device_id={"band": lax.rem(me + s, n)}, device_id_type=MESH
        )
        return carry

    lax.fori_loop(1, n, greet, 0)
    own = pltpu.make_async_copy(columns(me), band(own_ref, me), own_sem)
    own.start()
    pl.semaphore_wait(barrier, n - 1)

    def copy(s, source):
        peer = lax.rem(me + s, n)
        return pltpu.make_async_remote_copy(
            src_ref=columns(peer),
            dst_ref=band(own_ref, source),
            send_sem=send_sem.at[s],
            recv_sem=recv_sem.at[s],
            device_id={"band": peer},
            device_id_type=MESH,
        )

    def hand_over(source):
        return pltpu.make_async_remote_copy(
            src_ref=band(own_ref, source),
            dst_ref=band(other_ref, source),
            send_sem=pass_send.at[source],
            recv_sem=pass_recv.at[source],
            device_id=partner,
            device_id_type=MESH,
        )

    def start(s, carry):
        copy(s, me).start()
        return carry

    def arrive(s, carry):
        source = lax.rem(me - s + n, n)
        copy(s, source).wait_recv()
        hand_over(source).start()
        return carry

    def finish(s, carry):
        copy(s, me).wait_send()
        hand_over(lax.rem(me + s, n)).wait()
        return carry

    lax.fori_loop(1, n, start, 0)
    own.wait()
    hand_over(me).start()
    lax.fori_loop(1, n, arrive, 0)
    lax.fori_loop(1, n, finish, 0)
    hand_over(me).wait()


def exchange(x, n):
    rows, cols = x.shape
    shape = jax.ShapeDtypeStruct((rows * n, cols // n), x.dtype)
    vmem = pl.BlockSpec(memory_space=pltpu.VMEM)
    return pl.pallas_call(
        functools.partial(exchange_kernel, n),
        out_shape=(shape, shape),
        in_specs=[pl.BlockSpec(memory_space=pl.ANY)],
        out_specs=(vmem, vmem),
        scratch_shapes=[pltpu.SemaphoreType.DMA((n,))] * 4 + [pltpu.SemaphoreType.DMA],
        compiler_params=pltpu.CompilerParams(
            collective_id=0, has_side_effects=True, vmem_limit_bytes=48 << 20
        ),
        name="exchange",
    )(x)


CORES, YS, XS, ZS = 2, 4, 4, 8
EARLY, LATE = 0, 1
TOTAL = (256, 320)
HALF = tuple(t // 2 for t in TOTAL)
FIRST = tuple(t // 8 for t in TOTAL)
SECOND = tuple(t // 32 for t in TOTAL)
Z_USED = (8, 5)
CHUNK = tuple(t // z for t, z in zip(SECOND, Z_USED))
COPIES = 30


def coordinates():
    band, ga = lax.axis_index("band"), lax.axis_index("ga")
    core, y = lax.rem(band, CORES), lax.rem(band // CORES, YS)
    x = (band // (CORES * YS)) * 2 + lax.rem(ga, 2)
    return core, x, y, ga // 2


def device(core, x, y, z):
    return {"band": ((x // 2) * YS + y) * CORES + core, "ga": z * 2 + lax.rem(x, 2)}


class Summing:
    def __init__(self, group, p_ref, g_ref, scratch, send, recv):
        self.group, self.p_ref, self.g_ref = group, p_ref, g_ref
        self.acc2, self.acc3, self.got1, self.got2, self.got3 = scratch
        self.send, self.recv = send, recv
        core, x, y, z = self.at = coordinates()
        self.core, self.z = core, z
        self.a = jnp.where(core == 0, y, x)
        self.b = jnp.where(core == 0, x, y)
        self.partner = device(1 - core, x, y, z)
        self.from_p = group * HALF[EARLY]
        base = group * TOTAL[EARLY]
        self.half = base + core * HALF[group]
        self.first = self.half + self.a * FIRST[group]
        self.second = self.first + self.b * SECOND[group]
        self.other_half = base + (1 - core) * HALF[group]
        self.started = []

    def along(self, stage, s):
        core, x, y, z = self.at
        if stage == "z":
            to = lax.rem(z + s, ZS)
            return to, device(core, x, y, to)
        at = self.a if stage == "first" else self.b
        to = lax.rem(at + s, 4)
        on_y = core == (0 if stage == "first" else 1)
        return to, device(core, jnp.where(on_y, x, to), jnp.where(on_y, to, y), z)

    def copy(self, src, dst, index, peer):
        return pltpu.make_async_remote_copy(
            src_ref=src,
            dst_ref=dst,
            send_sem=self.send.at[self.group * COPIES + index],
            recv_sem=self.recv.at[self.group * COPIES + index],
            device_id=peer,
            device_id_type=MESH,
        )

    def start(self, src, dst, index, peer):
        self.copy(src, dst, index, peer).start()
        self.started.append((src.shape[0], index))

    def chunk(self, at, size):
        return self.g_ref.at[pl.ds(at, size)]

    def takes(self, z, then):
        if Z_USED[self.group] == ZS:
            then()
        else:
            pl.when(z < Z_USED[self.group])(then)

    def stage0(self):
        size = FIRST[self.group]
        for s in (2, 1, 3):
            to, peer = self.along("first", s)
            self.start(self.p_ref.at[pl.ds(self.from_p + to * size, size)], self.got1.at[s - 1], s - 1, peer)

    def stage1(self):
        size, step = FIRST[self.group], 8
        for s in range(3):
            self.copy(self.got1.at[s], self.got1.at[s], s, self.partner).wait_recv()

        def add(t, carry):
            at = pl.ds(t * step, step)
            own = self.p_ref[pl.ds(self.from_p + self.a * size + t * step, step)]
            self.acc2[at] = (own + self.got1[0, at]) + (self.got1[1, at] + self.got1[2, at])
            return carry

        lax.fori_loop(0, size // step, add, 0)
        size = SECOND[self.group]
        for s in (2, 1, 3):
            to, peer = self.along("second", s)
            self.start(self.acc2.at[pl.ds(to * size, size)], self.got2.at[s - 1], 2 + s, peer)

    def stage2(self):
        size = SECOND[self.group]
        for s in range(3):
            self.copy(self.got2.at[s], self.got2.at[s], 3 + s, self.partner).wait_recv()
        own = self.acc2[pl.ds(self.b * size, size)]
        self.acc3[...] = (own + self.got2[0]) + (self.got2[1] + self.got2[2])
        size = CHUNK[self.group]
        for s in (4, 3, 5, 2, 6, 1, 7):
            to, peer = self.along("z", s)

            def send():
                self.copy(self.acc3.at[pl.ds(to * size, size)], self.got3.at[s - 1], 5 + s, peer).start()

            self.takes(to, send)

    def stage3(self):
        size = CHUNK[self.group]
        own = self.second + self.z * size

        def total():
            for s in range(1, ZS):
                self.copy(self.got3.at[s - 1], self.got3.at[s - 1], 5 + s, self.partner).wait_recv()
            terms = [self.acc3[pl.ds(self.z * size, size)]] + [self.got3[s] for s in range(ZS - 1)]
            self.g_ref[pl.ds(own, size)] = tree(terms)
            for s in (4, 3, 5, 2, 6, 1, 7):
                to, peer = self.along("z", s)
                self.copy(self.chunk(own, size), self.chunk(own, size), 12 + s, peer).start()

        self.takes(self.z, total)

    def stage4(self):
        size = CHUNK[self.group]
        for s in range(1, ZS):
            sender = lax.rem(self.z + ZS - s, ZS)

            def receive():
                got = self.chunk(self.second + sender * size, size)
                self.copy(got, got, 12 + s, self.partner).wait_recv()

            self.takes(sender, receive)
        mine = self.chunk(self.second, SECOND[self.group])
        for s in (2, 1, 3):
            to, peer = self.along("second", s)
            self.start(mine, mine, 19 + s, peer)

    def stage5(self):
        size = SECOND[self.group]
        for s in range(1, 4):
            got = self.chunk(self.first + lax.rem(self.b + 4 - s, 4) * size, size)
            self.copy(got, got, 19 + s, self.partner).wait_recv()
        mine = self.chunk(self.first, FIRST[self.group])
        for s in (2, 1, 3):
            to, peer = self.along("first", s)
            self.start(mine, mine, 22 + s, peer)
        self.start(mine, mine, 26, self.partner)

    def stage6(self):
        size = FIRST[self.group]
        for s in (1, 3, 2):
            got = self.chunk(self.half + lax.rem(self.a + 4 - s, 4) * size, size)
            self.copy(got, got, 22 + s, self.partner).wait_recv()
            self.start(got, got, 26 + s, self.partner)

    def stage7(self):
        size = FIRST[self.group]
        for s in range(4):
            got = self.chunk(self.other_half + lax.rem(self.b + 4 - s, 4) * size, size)
            self.copy(got, got, 26 + s, self.partner).wait_recv()

    def finish(self):
        for size, index in self.started:
            part = self.chunk(0, size)
            self.copy(part, part, index, self.partner).wait_send()
        size = CHUNK[self.group]
        for s in range(1, ZS):
            to, peer = self.along("z", s)

            def sent():
                part = self.acc3.at[pl.ds(to * size, size)]
                self.copy(part, part, 5 + s, peer).wait_send()

            self.takes(to, sent)

            def sent_back():
                part = self.chunk(self.second, size)
                self.copy(part, part, 12 + s, peer).wait_send()

            self.takes(self.z, sent_back)


def orthonormalize_kernel(
    n, p_ref, c_ref, out_ref, g_ref, a_ref, z_ref, x_ref, hi_ref, lo_ref, lane_ref, row_ref, *rest
):
    early_scratch, late_scratch, (send, recv, send_sem, recv_sem, own_sem) = rest[:5], rest[5:10], rest[10:]
    width = c_ref.shape[1]
    rows_each = out_ref.shape[0]
    bands = n * B // rows_each
    per_panel = B // rows_each
    tiles = B // V
    me = lax.axis_index("band")
    core, x, y, z = coordinates()

    barrier = pltpu.get_barrier_semaphore()

    def greet(s, carry):
        pl.semaphore_signal(
            barrier, inc=1, device_id={"band": lax.rem(me + s, bands)}, device_id_type=MESH
        )
        return carry

    lax.fori_loop(1, bands, greet, 0)
    others = [device(core, lax.rem(x + s, XS), y, z) for s in (1, 3)]
    others += [device(core, x, y, lax.rem(z + s, ZS)) for s in range(1, ZS)]
    for peer in others:
        pl.semaphore_signal(barrier, inc=1, device_id=peer, device_id_type=MESH)
    pl.semaphore_wait(barrier, bands - 1 + len(others))

    early = Summing(EARLY, p_ref, g_ref, early_scratch, send, recv)
    late = Summing(LATE, p_ref, g_ref, late_scratch, send, recv)
    early.stage0()
    late.stage0()
    early.stage1()
    early.stage2()
    late.stage1()
    early.stage3()
    late.stage2()
    early.stage4()
    late.stage3()
    early.stage5()
    late.stage4()
    early.stage6()
    late.stage5()
    early.stage7()

    order = [block for group in grouped_blocks(n) for block in group]
    sub = lax.broadcasted_iota(jnp.int32, (V, B), 0)
    lane = lax.broadcasted_iota(jnp.int32, (V, B), 1)

    def load(panels):
        for i in panels:
            for j in range(i, n):
                at = order.index((i, j)) * tiles
                a_ref[i, :, j * B : (j + 1) * B] = g_ref[at : at + tiles].reshape(B, B)
            a_ref[i, :, n * B :] = c_ref[i * B : (i + 1) * B, :]
            at = order.index((i, i)) * tiles
            on_diagonal = [jnp.where(lane == q * V + sub, g_ref[at + q], 0.0) for q in range(tiles)]
            diagonal = jnp.sum(tree(on_diagonal), axis=0, keepdims=True)
            scale = jnp.broadcast_to(lax.rsqrt(diagonal), (V, B))
            lane_ref[i] = scale
            for q in range(tiles):
                row_ref[i, q * V : (q + 1) * V, :] = jnp.take_along_axis(scale, q * V + sub, axis=1)

    def remote(peer, sender):
        return pltpu.make_async_remote_copy(
            src_ref=x_ref.at[pl.ds(peer * rows_each, rows_each), :],
            dst_ref=out_ref.at[:, pl.ds(pl.multiple_of(sender * width, width), width)],
            send_sem=send_sem.at[peer],
            recv_sem=recv_sem.at[sender],
            device_id={"band": peer},
            device_id_type=MESH,
        )

    own = pltpu.make_async_copy(
        x_ref.at[pl.ds(me * rows_each, rows_each), :],
        out_ref.at[:, pl.ds(pl.multiple_of(me * width, width), width)],
        own_sem,
    )

    load([0, 1])

    def step(i, carry):
        @pl.when(i == 1)
        def _():
            late.stage6()

        @pl.when(i == 2)
        def _():
            late.stage7()
            load(range(2, n))
            for j in range(2, n):
                high, low = [hi_ref[k] for k in range(2)], [lo_ref[k] for k in range(2)]
                left = tuple(jnp.concatenate([h[:, j * B : (j + 1) * B] for h in part]) for part in (high, low))
                right = tuple(jnp.concatenate([h[:, j * B :] for h in part]) for part in (high, low))
                a_ref[j, :, j * B :] -= dot3(left, right, ((0,), (0,)))

        here = pl.multiple_of(i * B, B)
        lanes = lane_ref[i]
        rows = [
            a_ref[i, q * V : (q + 1) * V, pl.ds(here, B)] * row_ref[i, q * V : (q + 1) * V, :] * lanes
            for q in range(tiles)
        ]
        for q, inverse in enumerate(factor_inverse(rows)):
            z_ref[q * V : (q + 1) * V, :] = inverse * lanes
        for k in range(n):

            @pl.when(i == k)
            def _():
                panel = dot3(split(z_ref[...]), split(a_ref[k, :, (k + 1) * B :]), ((1,), (0,)))
                x_ref[k * B : (k + 1) * B, :] = panel[:, panel.shape[1] - width :]
                for peer in range(k * per_panel, (k + 1) * per_panel):

                    @pl.when(peer != me)
                    def _():
                        remote(peer, me).start()

                    @pl.when(peer == me)
                    def _():
                        own.start()

                high, low = split(panel)
                if k < 2:
                    hi_ref[k, :, (k + 1) * B :] = high
                    lo_ref[k, :, (k + 1) * B :] = low
                for j in range(k + 1, 2 if k < 2 else n):
                    at_j = (j - k - 1) * B
                    left = (high[:, at_j : at_j + B], low[:, at_j : at_j + B])
                    right = (high[:, at_j:], low[:, at_j:])
                    a_ref[j, :, j * B :] -= dot3(left, right, ((0,), (0,)))

        return carry

    lax.fori_loop(0, n, step, 0)
    early.finish()
    late.finish()
    own.wait()
    for other in range(bands):

        @pl.when(other != me)
        def _():
            remote(other, me).wait_send()
            remote(other, other).wait_recv()


def orthonormalize(p, c, bands):
    rows, width = c.shape
    n = rows // B
    vmem = pl.BlockSpec(memory_space=pltpu.VMEM)
    tiles = lambda *shape: pltpu.VMEM((*shape, V, B), jnp.float32)
    summing = []
    for g in (EARLY, LATE):
        summing += [tiles(FIRST[g]), tiles(SECOND[g]), tiles(3, FIRST[g]), tiles(3, SECOND[g])]
        summing += [tiles(ZS - 1, CHUNK[g])]
    return pl.pallas_call(
        functools.partial(orthonormalize_kernel, n),
        out_shape=jax.ShapeDtypeStruct((rows // bands, width * bands), jnp.float32),
        in_specs=[vmem, vmem],
        out_specs=vmem,
        scratch_shapes=[
            tiles(sum(TOTAL)),
            pltpu.VMEM((n, B, n * B + width), jnp.float32),
            pltpu.VMEM((B, B), jnp.float32),
            pltpu.VMEM((rows, width), jnp.float32),
            pltpu.VMEM((2, B, n * B + width), jnp.bfloat16),
            pltpu.VMEM((2, B, n * B + width), jnp.bfloat16),
            tiles(n),
            pltpu.VMEM((n, B, B), jnp.float32),
            *summing,
            pltpu.SemaphoreType.DMA((2 * COPIES,)),
            pltpu.SemaphoreType.DMA((2 * COPIES,)),
            pltpu.SemaphoreType.DMA((bands,)),
            pltpu.SemaphoreType.DMA((bands,)),
            pltpu.SemaphoreType.DMA,
        ],
        compiler_params=pltpu.CompilerParams(
            collective_id=1, has_side_effects=True, vmem_limit_bytes=48 << 20
        ),
        name="orthonormalize",
    )(p, c)


def local(coeffs):
    bands = lax.axis_size("band")
    columns_all = coeffs.shape[1] * lax.axis_size("ga")
    own, other = exchange(coeffs, bands)
    return orthonormalize(gram(own, other, columns_all), own, bands)


def solution(mesh):
    return jax.shard_map(
        local,
        mesh=mesh,
        in_specs=(P("band", "ga"),),
        out_specs=P("band", "ga"),
        check_vma=False,
    )
```

time: 709 us -> 109 us (0.15); the launches traced: 698 us -> 108 us
  waiting for transfers between devices: 314 us -> 0 us
  other arithmetic: 261 us -> 0 us
  Pallas kernels: 0 us -> 105 us
  matrix products: 71.1 us -> 0 us
  local copies, waits for them, and re-layouts: 32.8 us -> 2.2 us
  between operations: 19 us -> 0.03 us
    another operation x33 -> x0, other arithmetic: 256 us -> none  [the longest x30 172 us: local(): factor = jnp.linalg.cholesky(margin)]
    all_gather x2 -> x0, waiting for transfers between devices: 185 us -> none  [the longest x1 116 us: local(): gathered = lax.all_gather(coeffs, 'band', axis=0, tiled=True)]
    psum x1 -> x0, waiting for transfers between devices: 128 us -> none  [local(): summed = lax.psum(partial_value, 'ga')]
    pallas_call x0 -> x3, Pallas kernels: none -> 105 us  [the longest x1 80.1 us: orthonormalize(): pl.pallas_call(functools.partial(orthonormalize_kernel, n), out_shape=jax...]
    another operation x29 -> x0, matrix products: 36 us -> none  [the longest x14 23.1 us: local(): factor = jnp.linalg.cholesky(margin)]
    dot_general x2 -> x0, matrix products: 35.1 us -> none  [the longest x1 20.5 us: local(): jnp.dot(coeffs, gathered.T, precision=lax.Precision.HIGHEST, preferred_el...]
    another operation x37 -> x0, local copies, waits for them, and re-layouts: 25.3 us -> none
  transfers between devices with their start and end apart: 3 -> 0, of which waited for: 3 -> 0; matrix products, arithmetic and copies ran while one was open for 0% -> 0% of each run, Pallas kernels for 0% -> 0%
where the time goes in v3:
time: 109 us; the launch traced here: 108 us
  Pallas kernels  105 us (96%)
  local copies, waits for them, and re-layouts  2.2 us (2%)
    pallas_call x1, Pallas kernels, orthonormalize(): pl.pallas_call(functools.partial(orthonormalize_kernel, n), out_shape=jax...  80.1 us
    pallas_call x1, Pallas kernels, exchange(): pl.pallas_call(functools.partial(exchange_kernel, n), out_shape=(shape, s...  22.7 us
    pallas_call x1, Pallas kernels, gram(): pl.pallas_call(functools.partial(gram_kernel, n, 1.0 / columns_all), out_...  2.67 us
    unnamed x3, local copies, waits for them, and re-layouts  2.2 us

profile of v3, /device:TPU:29, one launch (start us, length us, event | category | flops | bytes accessed | tf_op | source)
XLA Modules:
  0.0 107.6 jit_solution(5193758945287932866)
XLA Ops:
  0.0 0.0 copy-start
  0.0 1.2 %copy-done = f32[64,4096]{1,0:T(8,128)S(1)} copy-done((f32[64,4096]{1,0:T(8,128)S(1)}, f32[64,4096]{1,0:T(8,128)}, u32[]{:S(2)}) %copy-start) | copy-done | bytes 1048600
  1.2 22.7 %exchange.1 = (f32[1024,256]{1,0:T(8,128)S(1)}, f32[1024,256]{1,0:T(8,128)S(1)}) custom-call(f32[64,4096]{1,0:T(8,128)S(1)} %copy-done), custom_call_target="tpu_custom_call" | custom-call | tf_op jit(solution)/shard_map/exchange/pallas_call | solution.py:229
  23.9 2.7 %gram.1.p_ref = f32[288,8,128]{2,1,0:T(8,128)S(1)} custom-call(f32[1024,256]{1,0:T(8,128)S(1)} %get-tuple-element.7.own_ref.c_ref, f32[1024,256]{1,0:T(8,128)S(1)} %get-tuple-element.8.other_ref), custom_call_target="tpu_custom_call" | custom-call | tf_op jit(solution)/shard_map/gram/pallas_call | solution.py:146
  26.6 80.1 %orthonormalize.1 = f32[64,4096]{1,0:T(8,128)S(1)} custom-call(f32[288,8,128]{2,1,0:T(8,128)S(1)} %gram.1.p_ref, f32[1024,256]{1,0:T(8,128)S(1)} %get-tuple-element.7.own_ref.c_ref), custom_call_target="tpu_custom_call" | custom-call | tf_op jit(solution)/shard_map/orthonormalize/pallas_call | solution.py:580
  106.7 1.0 copy.3
Async XLA Ops:
  0.0 1.2 %copy-start = (f32[64,4096]{1,0:T(8,128)S(1)}, f32[64,4096]{1,0:T(8,128)}, u32[]{:S(2)}) copy-start(f32[64,4096]{1,0:T(8,128)} %src_ref.1) | copy-start | bytes 3145732

commit v4 on v3

v4 whole, which is shorter than its diff:
```python
import functools

import jax
import jax.numpy as jnp
from jax import lax
from jax.experimental import pallas as pl
from jax.experimental.pallas import tpu as pltpu
from jax.sharding import PartitionSpec as P

MESH = pl.DeviceIdType.MESH

B = 128
V = 8


def split(x):
    hi = x.astype(jnp.bfloat16)
    return hi, (x - hi.astype(jnp.float32)).astype(jnp.bfloat16)


def dot3(a, b, dims):
    (ca,), (cb,) = dims
    ah, al = a
    bh, bl = b
    left = jnp.concatenate([ah, al, ah], axis=ca)
    right = jnp.concatenate([bh, bh, bl], axis=cb)
    return lax.dot_general(left, right, (dims, ((), ())), preferred_element_type=jnp.float32)


def lane_col(t, c):
    return jnp.take_along_axis(t, jnp.full((V, B), c, jnp.int32), axis=1)


def sub_row(t, k):
    return jnp.broadcast_to(t[k : k + 1, :], (V, B))


def tree(m):
    while len(m) > 1:
        m = [m[e] + m[e + 1] if e + 1 < len(m) else m[e] for e in range(0, len(m), 2)]
    return m[0]


def factor_inverse(rows):
    n = len(rows)
    rows = list(rows)
    sub = lax.broadcasted_iota(jnp.int32, (V, B), 0)
    lane = lax.broadcasted_iota(jnp.int32, (V, B), 1)
    out = []
    cols = [lane_col(rows[0], k) for k in range(V)]
    for p in range(n):
        c0 = p * V
        last = p == n - 1
        in_block = (lane >= c0) & (lane < c0 + V)
        t = jnp.where(in_block, jnp.where(lane - c0 == sub, 1.0, 0.0), rows[p])
        f = jnp.where(lane < c0 + V, t, 0.0)
        pivots = None
        below_m = {q: [lane_col(rows[q], c0 + k) for k in range(V)] for q in range(p + 1, n)}
        if not last:
            a = list(below_m[p + 1])
            ahead = [lane_col(rows[p + 1], c0 + V + k) for k in range(V)]
        for k in range(0, V, 2):
            h1, h2 = sub == k, sub == k + 1
            here = h1 | h2
            d11, d12, d22 = sub_row(cols[k], k), sub_row(cols[k + 1], k), sub_row(cols[k + 1], k + 1)
            det = d11 * d22 - d12 * d12
            r = 1.0 / det
            m1, m2 = jnp.where(here, 0.0, cols[k]), jnp.where(here, 0.0, cols[k + 1])

            def solve(col):
                v1, v2 = sub_row(col, k), sub_row(col, k + 1)
                return (d22 * v1 - d12 * v2) * r, (d11 * v2 - d12 * v1) * r

            def eliminate(col):
                u1, u2 = solve(col)
                return jnp.where(h1, u1, jnp.where(h2, u2, col - (m1 * u1 + m2 * u2))), u1, u2

            for j in range(k + 2, V):
                cols[j], u1, u2 = eliminate(cols[j])
                if not last:
                    a[j] = a[j] - (a[k] * u1 + a[k + 1] * u2)
            if not last:
                s1 = (d22 * a[k] - d12 * a[k + 1]) * r
                s2 = (d11 * a[k + 1] - d12 * a[k]) * r
                for j in range(V):
                    ahead[j] = ahead[j] - (s1 * sub_row(a[k], j) + s2 * sub_row(a[k + 1], j))
            q = 1.0 / d11
            ratio = d12 * q
            f1 = sub_row(f, k)
            f2 = sub_row(f, k + 1) - ratio * f1
            g2 = d11 * r
            g1 = q
            below = sub > k + 1
            b1 = jnp.where(below, cols[k], 0.0)
            b2 = jnp.where(below, cols[k + 1], 0.0)
            l2 = b2 - b1 * ratio
            f = jnp.where(h2, f2, f - b1 * (f1 * g1) - l2 * (f2 * g2))
            t, _, _ = eliminate(t)
            scale = jnp.where(h1, g1, g2)
            pivots = scale if pivots is None else jnp.where(here, scale, pivots)
        out.append(f * jnp.sqrt(pivots))
        if last:
            break
        cols = ahead
        w = [sub_row(t, k) for k in range(V)]
        for q in range(p + 1, n):
            acc = jnp.where(in_block, 0.0, rows[q])
            rows[q] = acc - tree([below_m[q][k] * w[k] for k in range(V)])
    return out


CORES, YS, XS, ZS = 2, 4, 4, 8
TOTAL = (128, 128, 320)
HALF = tuple(t // 2 for t in TOTAL)
FIRST = tuple(t // 8 for t in TOTAL)
SECOND = tuple(t // 32 for t in TOTAL)
Z_USED = (0, 0, 5)
CHUNK = tuple(t // max(z, 1) for t, z in zip(SECOND, Z_USED))
COPIES = 30


def grouped_blocks(n):
    first = [(0, j) for j in range(n)]
    second = [(1, j) for j in range(1, n)] + [(2, 2)]
    rest = [(i, j) for i in range(2, n) for j in range(i, n) if (i, j) != (2, 2)]
    return first, second, rest


def coordinates():
    band, ga = lax.axis_index("band"), lax.axis_index("ga")
    core, y = lax.rem(band, CORES), lax.rem(band // CORES, YS)
    x = (band // (CORES * YS)) * 2 + lax.rem(ga, 2)
    return core, x, y, ga // 2


def device(core, x, y, z):
    return {"band": ((x // 2) * YS + y) * CORES + core, "ga": z * 2 + lax.rem(x, 2)}


class Summing:
    def __init__(self, group, p_ref, g_ref, scratch, send, recv):
        self.group, self.p_ref, self.g_ref = group, p_ref, g_ref
        self.acc2, self.acc3, self.got1, self.got2, self.got3 = scratch
        self.send, self.recv = send, recv
        self.direct = Z_USED[group] == 0
        core, x, y, z = self.at = coordinates()
        self.core, self.z = core, z
        self.a = jnp.where(core == 0, y, x)
        self.b = jnp.where(core == 0, x, y)
        self.partner = device(1 - core, x, y, z)
        self.from_p = sum(HALF[:group])
        base = sum(TOTAL[:group])
        self.half = base + core * HALF[group]
        self.first = self.half + self.a * FIRST[group]
        self.second = self.first + self.b * SECOND[group]
        self.other_half = base + (1 - core) * HALF[group]
        self.started = []

    def along(self, stage, s):
        core, x, y, z = self.at
        if stage == "z":
            to = lax.rem(z + s, ZS)
            return to, device(core, x, y, to)
        at = self.a if stage == "first" else self.b
        to = lax.rem(at + s, 4)
        on_y = core == (0 if stage == "first" else 1)
        return to, device(core, jnp.where(on_y, x, to), jnp.where(on_y, to, y), z)

    def copy(self, src, dst, index, peer):
        return pltpu.make_async_remote_copy(
            src_ref=src,
            dst_ref=dst,
            send_sem=self.send.at[self.group * COPIES + index],
            recv_sem=self.recv.at[self.group * COPIES + index],
            device_id=peer,
            device_id_type=MESH,
        )

    def start(self, src, dst, index, peer):
        self.copy(src, dst, index, peer).start()
        self.started.append((src.shape[0], index))

    def chunk(self, at, size):
        return self.g_ref.at[pl.ds(at, size)]

    def takes(self, z, then):
        if Z_USED[self.group] == ZS:
            then()
        else:
            pl.when(z < Z_USED[self.group])(then)

    def stage0(self):
        size = FIRST[self.group]
        for s in (2, 1, 3):
            to, peer = self.along("first", s)
            self.start(self.p_ref.at[pl.ds(self.from_p + to * size, size)], self.got1.at[s - 1], s - 1, peer)

    def stage1(self):
        size, step = FIRST[self.group], 8
        for s in range(3):
            self.copy(self.got1.at[s], self.got1.at[s], s, self.partner).wait_recv()

        def add(t, carry):
            at = pl.ds(t * step, step)
            own = self.p_ref[pl.ds(self.from_p + self.a * size + t * step, step)]
            self.acc2[at] = (own + self.got1[0, at]) + (self.got1[1, at] + self.got1[2, at])
            return carry

        lax.fori_loop(0, size // step, add, 0)
        size = SECOND[self.group]
        for s in (2, 1, 3):
            to, peer = self.along("second", s)
            self.start(self.acc2.at[pl.ds(to * size, size)], self.got2.at[s - 1], 2 + s, peer)

    def across_z(self):
        size = SECOND[self.group]
        self.got3[pl.ds(self.z, 1)] = self.acc3[...][None]
        for s in (4, 3, 5, 2, 6, 1, 7):
            to, peer = self.along("z", s)
            self.start(self.acc3, self.got3.at[self.z], 5 + s, peer)

    def stage2(self):
        size = SECOND[self.group]
        for s in range(3):
            self.copy(self.got2.at[s], self.got2.at[s], 3 + s, self.partner).wait_recv()
        own = self.acc2[pl.ds(self.b * size, size)]
        self.acc3[...] = (own + self.got2[0]) + (self.got2[1] + self.got2[2])
        if self.direct:
            self.across_z()
            return
        size = CHUNK[self.group]
        for s in (4, 3, 5, 2, 6, 1, 7):
            to, peer = self.along("z", s)

            def send():
                self.copy(self.acc3.at[pl.ds(to * size, size)], self.got3.at[s - 1], 5 + s, peer).start()

            self.takes(to, send)

    def stage3(self):
        if self.direct:
            for s in range(1, ZS):
                self.copy(self.acc3, self.got3.at[0], 5 + s, self.partner).wait_recv()
            self.g_ref[pl.ds(self.second, SECOND[self.group])] = tree([self.got3[k] for k in range(ZS)])
            self.back()
            return
        size = CHUNK[self.group]
        own = self.second + self.z * size

        def total():
            for s in range(1, ZS):
                self.copy(self.got3.at[s - 1], self.got3.at[s - 1], 5 + s, self.partner).wait_recv()
            terms = [self.acc3[pl.ds(self.z * size, size)]] + [self.got3[s] for s in range(ZS - 1)]
            self.g_ref[pl.ds(own, size)] = tree(terms)
            for s in (4, 3, 5, 2, 6, 1, 7):
                to, peer = self.along("z", s)
                self.copy(self.chunk(own, size), self.chunk(own, size), 12 + s, peer).start()

        self.takes(self.z, total)

    def stage4(self):
        size = CHUNK[self.group]
        for s in range(1, ZS):
            sender = lax.rem(self.z + ZS - s, ZS)

            def receive():
                got = self.chunk(self.second + sender * size, size)
                self.copy(got, got, 12 + s, self.partner).wait_recv()

            self.takes(sender, receive)
        self.back()

    def back(self):
        mine = self.chunk(self.second, SECOND[self.group])
        for s in (2, 1, 3):
            to, peer = self.along("second", s)
            self.start(mine, mine, 19 + s, peer)

    def stage5(self):
        size = SECOND[self.group]
        for s in range(1, 4):
            got = self.chunk(self.first + lax.rem(self.b + 4 - s, 4) * size, size)
            self.copy(got, got, 19 + s, self.partner).wait_recv()
        mine = self.chunk(self.first, FIRST[self.group])
        for s in (2, 1, 3):
            to, peer = self.along("first", s)
            self.start(mine, mine, 22 + s, peer)
        self.start(mine, mine, 26, self.partner)

    def stage6(self):
        size = FIRST[self.group]
        for s in (1, 3, 2):
            got = self.chunk(self.half + lax.rem(self.a + 4 - s, 4) * size, size)
            self.copy(got, got, 22 + s, self.partner).wait_recv()
            self.start(got, got, 26 + s, self.partner)

    def stage7(self):
        size = FIRST[self.group]
        for s in range(4):
            got = self.chunk(self.other_half + lax.rem(self.b + 4 - s, 4) * size, size)
            self.copy(got, got, 26 + s, self.partner).wait_recv()

    def finish(self):
        for size, index in self.started:
            part = self.chunk(0, size)
            self.copy(part, part, index, self.partner).wait_send()
        if self.direct:
            return
        size = CHUNK[self.group]
        for s in range(1, ZS):
            to, peer = self.along("z", s)

            def sent():
                part = self.acc3.at[pl.ds(to * size, size)]
                self.copy(part, part, 5 + s, peer).wait_send()

            self.takes(to, sent)

            def sent_back():
                part = self.chunk(self.second, size)
                self.copy(part, part, 12 + s, peer).wait_send()

            self.takes(self.z, sent_back)


def orthonormalize_kernel(n, scale, src_ref, out_ref, *scratch):
    (own_ref, other_ref, held_hi, held_lo, p_ref, g_ref, cur_ref, d_ref, z_ref, x_ref, hi_ref, lo_ref, lane_ref) = scratch[:13]
    groups_scratch = [scratch[13 + 5 * g : 18 + 5 * g] for g in range(3)]
    (send, recv, x_send, x_recv, in_send, in_recv, pass_send, pass_recv, own_sem) = scratch[28:]
    rows_each, width = src_ref.shape[0], own_ref.shape[1]
    bands = src_ref.shape[1] // width
    per_panel = B // rows_each
    tiles = B // V
    me = lax.axis_index("band")
    core, x, y, z = coordinates()
    partner = device(1 - core, x, y, z)

    barrier = pltpu.get_barrier_semaphore()

    def greet(s, carry):
        pl.semaphore_signal(
            barrier, inc=1, device_id={"band": lax.rem(me + s, bands)}, device_id_type=MESH
        )
        return carry

    others = [device(core, x, y, lax.rem(z + s, ZS)) for s in range(1, ZS)]
    others += [device(core, lax.rem(x + s, XS), y, z) for s in (1, 3)]
    for peer in others:
        pl.semaphore_signal(barrier, inc=1, device_id=peer, device_id_type=MESH)
    lax.fori_loop(1, bands, greet, 0)

    def columns(ref, index):
        return ref.at[:, pl.ds(pl.multiple_of(index * width, width), width)]

    def band(ref, index):
        return ref.at[pl.ds(pl.multiple_of(index * rows_each, rows_each), rows_each), :]

    mine = pltpu.make_async_copy(columns(src_ref, me), band(own_ref, me), own_sem)
    mine.start()
    pl.semaphore_wait(barrier, bands - 1 + len(others))

    def bring(s, source):
        peer = lax.rem(me + s, bands)
        return pltpu.make_async_remote_copy(
            src_ref=columns(src_ref, peer),
            dst_ref=band(own_ref, source),
            send_sem=in_send.at[s],
            recv_sem=in_recv.at[s],
            device_id={"band": peer},
            device_id_type=MESH,
        )

    def hand_over(source):
        return pltpu.make_async_remote_copy(
            src_ref=band(own_ref, source),
            dst_ref=band(other_ref, source),
            send_sem=pass_send.at[source],
            recv_sem=pass_recv.at[source],
            device_id=partner,
            device_id_type=MESH,
        )

    def keep(ref, source, at):
        rows = pl.ds(pl.multiple_of(source * rows_each, rows_each), rows_each)
        high, low = split(ref[rows, :])
        held_hi[rows, at : at + width] = high
        held_lo[rows, at : at + width] = low

    def start(s, carry):
        bring(s, me).start()
        return carry

    def arrive(s, carry):
        source = lax.rem(me - s + bands, bands)
        bring(s, source).wait_recv()
        hand_over(source).start()
        keep(own_ref, source, 0)
        return carry

    def finish(s, carry):
        source = lax.rem(me + 1 - 2 * core - s + bands, bands)
        hand_over(source).wait_recv()
        keep(other_ref, source, width)
        return carry

    def sent(s, carry):
        bring(s, me).wait_send()
        hand_over(lax.rem(me + s, bands)).wait_send()
        return carry

    lax.fori_loop(1, bands, start, 0)
    mine.wait()
    hand_over(me).start()
    keep(own_ref, me, 0)
    lax.fori_loop(1, bands, arrive, 0)
    lax.fori_loop(0, bands, finish, 0)

    groups = grouped_blocks(n)

    def multiply(g):
        half = len(groups[g]) // CORES
        for c in range(CORES):

            @pl.when(core == c)
            def _():
                blocks = groups[g][c * half : (c + 1) * half]
                for i in sorted({i for i, _ in blocks}):
                    wanted = [j for k, j in blocks if k == i]
                    first, end = min(wanted), max(wanted) + 1
                    left = (held_hi[i * B : (i + 1) * B], held_lo[i * B : (i + 1) * B])
                    right = (held_hi[first * B : end * B], held_lo[first * B : end * B])
                    out = dot3(left, right, ((1,), (1,))) * scale
                    for j in wanted:
                        at = sum(HALF[:g]) + blocks.index((i, j)) * tiles
                        block = out[:, (j - first) * B : (j - first + 1) * B]
                        p_ref[at : at + tiles] = block.reshape(tiles, V, B)

    one, two, three = (Summing(g, p_ref, g_ref, groups_scratch[g], send, recv) for g in range(3))
    multiply(0)
    one.stage0()
    multiply(1)
    two.stage0()
    multiply(2)
    three.stage0()
    one.stage1()
    two.stage1()
    one.stage2()
    three.stage1()
    two.stage2()
    one.stage3()
    three.stage2()
    two.stage3()
    one.stage5()
    three.stage3()
    two.stage5()
    one.stage6()
    three.stage4()
    two.stage6()
    one.stage7()
    three.stage5()

    order = [block for group in groups for block in group]
    sub = lax.broadcasted_iota(jnp.int32, (V, B), 0)
    lane = lax.broadcasted_iota(jnp.int32, (V, B), 1)

    def prepare(k):
        at = order.index((k, k)) * tiles
        on_diagonal = [jnp.where(lane == q * V + sub, g_ref[at + q], 0.0) for q in range(tiles)]
        diagonal = jnp.sum(tree(on_diagonal), axis=0, keepdims=True)
        lanes = jnp.broadcast_to(lax.rsqrt(diagonal), (V, B))
        lane_ref[...] = lanes
        taken = None
        if k:
            left = (hi_ref[: k * B, k * B : (k + 1) * B], lo_ref[: k * B, k * B : (k + 1) * B])
            right = (hi_ref[: k * B, k * B :], lo_ref[: k * B, k * B :])
            taken = dot3(left, right, ((0,), (0,)))
        for j in range(k, n + width // B):
            if j < n:
                at = order.index((k, j)) * tiles
                block = g_ref[at : at + tiles].reshape(B, B)
            else:
                block = own_ref[k * B : (k + 1) * B, (j - n) * B : (j - n + 1) * B]
            if k:
                block = block - taken[:, (j - k) * B : (j - k + 1) * B]
            if j > k:
                cur_ref[:, j * B : (j + 1) * B] = block
                continue
            for q in range(tiles):
                rows = jnp.take_along_axis(lanes, q * V + sub, axis=1)
                d_ref[q * V : (q + 1) * V, :] = block[q * V : (q + 1) * V] * rows * lanes

    def remote(peer, sender):
        return pltpu.make_async_remote_copy(
            src_ref=x_ref.at[pl.ds(peer * rows_each, rows_each), :],
            dst_ref=columns(out_ref, sender),
            send_sem=x_send.at[peer],
            recv_sem=x_recv.at[sender],
            device_id={"band": peer},
            device_id_type=MESH,
        )

    stays = pltpu.make_async_copy(band(x_ref, me), columns(out_ref, me), own_sem)

    def step(i, carry):
        for k in range(n):

            @pl.when(i == k)
            def _():
                if k == 1:
                    two.stage7()
                if k == 2:
                    three.stage7()
                prepare(k)

        rows = [d_ref[q * V : (q + 1) * V, :] for q in range(tiles)]
        lanes = lane_ref[...]
        for q, inverse in enumerate(factor_inverse(rows)):
            z_ref[q * V : (q + 1) * V, :] = inverse * lanes
        for k in range(n):

            @pl.when(i == k)
            def _():
                if k == 1:
                    three.stage6()
                panel = dot3(split(z_ref[...]), split(cur_ref[:, (k + 1) * B :]), ((1,), (0,)))
                x_ref[k * B : (k + 1) * B, :] = panel[:, panel.shape[1] - width :]
                for peer in range(k * per_panel, (k + 1) * per_panel):

                    @pl.when(peer != me)
                    def _():
                        remote(peer, me).start()

                    @pl.when(peer == me)
                    def _():
                        stays.start()

                if k < n - 1:
                    high, low = split(panel)
                    hi_ref[k * B : (k + 1) * B, (k + 1) * B :] = high
                    lo_ref[k * B : (k + 1) * B, (k + 1) * B :] = low

        return carry

    lax.fori_loop(0, n, step, 0)
    lax.fori_loop(1, bands, sent, 0)
    hand_over(me).wait_send()
    for group in (one, two, three):
        group.finish()
    stays.wait()
    for other in range(bands):

        @pl.when(other != me)
        def _():
            remote(other, me).wait_send()
            remote(other, other).wait_recv()


def orthonormalize(coeffs, bands, columns_all):
    rows_each, columns = coeffs.shape
    rows, width = rows_each * bands, columns // bands
    n = rows // B
    tiles = lambda *shape: pltpu.VMEM((*shape, V, B), jnp.float32)
    whole = n * B + width
    summing = []
    for g in range(3):
        summing += [tiles(FIRST[g]), tiles(SECOND[g]), tiles(3, FIRST[g]), tiles(3, SECOND[g])]
        summing += [tiles(ZS - 1, CHUNK[g]) if Z_USED[g] else tiles(ZS, SECOND[g])]
    return pl.pallas_call(
        functools.partial(orthonormalize_kernel, n, 1.0 / columns_all),
        out_shape=jax.ShapeDtypeStruct(coeffs.shape, jnp.float32),
        in_specs=[pl.BlockSpec(memory_space=pltpu.HBM)],
        out_specs=pl.BlockSpec(memory_space=pltpu.VMEM),
        scratch_shapes=[
            pltpu.VMEM((rows, width), jnp.float32),
            pltpu.VMEM((rows, width), jnp.float32),
            pltpu.VMEM((rows, CORES * width), jnp.bfloat16),
            pltpu.VMEM((rows, CORES * width), jnp.bfloat16),
            tiles(sum(HALF)),
            tiles(sum(TOTAL)),
            pltpu.VMEM((B, whole), jnp.float32),
            pltpu.VMEM((B, B), jnp.float32),
            pltpu.VMEM((B, B), jnp.float32),
            pltpu.VMEM((rows, width), jnp.float32),
            pltpu.VMEM((rows, whole), jnp.bfloat16),
            pltpu.VMEM((rows, whole), jnp.bfloat16),
            pltpu.VMEM((V, B), jnp.float32),
            *summing,
            pltpu.SemaphoreType.DMA((3 * COPIES,)),
            pltpu.SemaphoreType.DMA((3 * COPIES,)),
            *[pltpu.SemaphoreType.DMA((bands,))] * 6,
            pltpu.SemaphoreType.DMA,
        ],
        compiler_params=pltpu.CompilerParams(
            collective_id=0, has_side_effects=True, vmem_limit_bytes=40 << 20
        ),
        name="orthonormalize",
    )(coeffs)


def local(coeffs):
    bands = lax.axis_size("band")
    return orthonormalize(coeffs, bands, coeffs.shape[1] * lax.axis_size("ga"))


def solution(mesh):
    return jax.shard_map(
        local,
        mesh=mesh,
        in_specs=(P("band", "ga"),),
        out_specs=P("band", "ga"),
        check_vma=False,
    )
```

time: 109 us -> 104 us (0.954); the launches traced: 108 us -> 104 us
  Pallas kernels: 105 us -> 102 us
    pallas_call x3 -> x1, Pallas kernels: 105 us -> 102 us  [orthonormalize(): pl.pallas_call(functools.partial(orthonormalize_kernel, n, 1.0 / columns_...]
where the time goes in v4:
time: 104 us
  Pallas kernels  102 us (98%)
  local copies, waits for them, and re-layouts  2.2 us (2%)
    pallas_call x1, Pallas kernels, orthonormalize(): pl.pallas_call(functools.partial(orthonormalize_kernel, n, 1.0 / columns_...  102 us
    unnamed x3, local copies, waits for them, and re-layouts  2.2 us

profile of v4, /device:TPU:29, one launch (start us, length us, event | category | flops | bytes accessed | tf_op | source)
XLA Modules:
  0.0 104.1 jit_solution(14065967435706022232)
XLA Ops:
  0.0 0.0 copy-start
  0.0 1.2 %copy-done = f32[64,4096]{1,0:T(8,128)S(1)} copy-done((f32[64,4096]{1,0:T(8,128)S(1)}, f32[64,4096]{1,0:T(8,128)}, u32[]{:S(2)}) %copy-start) | copy-done | bytes 1048600
  1.2 101.9 %orthonormalize.1 = f32[64,4096]{1,0:T(8,128)S(1)} custom-call(f32[64,4096]{1,0:T(8,128)S(1)} %copy-done), custom_call_target="tpu_custom_call" | custom-call | tf_op jit(solution)/shard_map/orthonormalize/pallas_call | solution.py:568
  103.1 1.0 copy.3
Async XLA Ops:
  0.0 1.2 %copy-start = (f32[64,4096]{1,0:T(8,128)S(1)}, f32[64,4096]{1,0:T(8,128)}, u32[]{:S(2)}) copy-start(f32[64,4096]{1,0:T(8,128)} %src_ref.1) | copy-start | bytes 3145732

commit v5 on v4

--- a/solution.py
+++ b/solution.py
@@ -110,19 +110,19 @@
 
 
 CORES, YS, XS, ZS = 2, 4, 4, 8
-TOTAL = (128, 128, 320)
+TOTAL = (128, 224, 224)
 HALF = tuple(t // 2 for t in TOTAL)
 FIRST = tuple(t // 8 for t in TOTAL)
 SECOND = tuple(t // 32 for t in TOTAL)
-Z_USED = (0, 0, 5)
+Z_USED = (0, 0, 7)
 CHUNK = tuple(t // max(z, 1) for t, z in zip(SECOND, Z_USED))
 COPIES = 30
 
 
 def grouped_blocks(n):
     first = [(0, j) for j in range(n)]
-    second = [(1, j) for j in range(1, n)] + [(2, 2)]
-    rest = [(i, j) for i in range(2, n) for j in range(i, n) if (i, j) != (2, 2)]
+    second = [(i, j) for i in (1, 2) for j in range(i, n)] + [(3, 3)]
+    rest = [(i, j) for i in range(3, n) for j in range(i, n) if (i, j) != (3, 3)]
     return first, second, rest
 
 
@@ -196,7 +196,7 @@
             self.start(self.p_ref.at[pl.ds(self.from_p + to * size, size)], self.got1.at[s - 1], s - 1, peer)
 
     def stage1(self):
-        size, step = FIRST[self.group], 8
+        size, step = FIRST[self.group], 4
         for s in range(3):
             self.copy(self.got1.at[s], self.got1.at[s], s, self.partner).wait_recv()
 
@@ -412,8 +412,8 @@
     mine.wait()
     hand_over(me).start()
     keep(own_ref, me, 0)
-    lax.fori_loop(1, bands, arrive, 0)
-    lax.fori_loop(0, bands, finish, 0)
+    lax.fori_loop(1, bands, lambda s, carry: finish(s - 1, arrive(s, carry)), 0)
+    finish(bands - 1, 0)
 
     groups = grouped_blocks(n)
 
@@ -455,9 +455,7 @@
     two.stage5()
     one.stage6()
     three.stage4()
-    two.stage6()
     one.stage7()
-    three.stage5()
 
     order = [block for group in groups for block in group]
     sub = lax.broadcasted_iota(jnp.int32, (V, B), 0)
@@ -508,7 +506,7 @@
             def _():
                 if k == 1:
                     two.stage7()
-                if k == 2:
+                if k == 3:
                     three.stage7()
                 prepare(k)
 
@@ -520,7 +518,10 @@
 
             @pl.when(i == k)
             def _():
-                if k == 1:
+                if k == 0:
+                    two.stage6()
+                    three.stage5()
+                if k == 2:
                     three.stage6()
                 panel = dot3(split(z_ref[...]), split(cur_ref[:, (k + 1) * B :]), ((1,), (0,)))
                 x_ref[k * B : (k + 1) * B, :] = panel[:, panel.shape[1] - width :]
@@ -591,7 +592,7 @@
             pltpu.SemaphoreType.DMA,
         ],
         compiler_params=pltpu.CompilerParams(
-            collective_id=0, has_side_effects=True, vmem_limit_bytes=40 << 20
+            collective_id=0, has_side_effects=True, vmem_limit_bytes=52 << 20
         ),
         name="orthonormalize",
     )(coeffs)

time: 104 us -> 99.2 us (0.954)
  Pallas kernels: 102 us -> 98.1 us
  local copies, waits for them, and re-layouts: 2.2 us -> 0.97 us
    pallas_call x1, Pallas kernels: 102 us -> 98.1 us  [orthonormalize(): pl.pallas_call(functools.partial(orthonormalize_kernel, n, 1.0 / columns_...]
    unnamed x3 -> x1, local copies, waits for them, and re-layouts: 2.2 us -> 0.97 us
where the time goes in v5:
time: 99.2 us; the launch traced here: 99.1 us
  Pallas kernels  98.1 us (99%)
    pallas_call x1, Pallas kernels, orthonormalize(): pl.pallas_call(functools.partial(orthonormalize_kernel, n, 1.0 / columns_...  98.1 us

profile of v5, /device:TPU:29, one launch (start us, length us, event | category | flops | bytes accessed | tf_op | source)
XLA Modules:
  0.0 99.1 jit_solution(767937311835775396)
XLA Ops:
  0.0 98.1 %orthonormalize.1 = f32[64,4096]{1,0:T(8,128)S(1)} custom-call(f32[64,4096]{1,0:T(8,128)} %src_ref.1), custom_call_target="tpu_custom_call" | custom-call | tf_op jit(solution)/shard_map/orthonormalize/pallas_call | solution.py:569
  98.1 1.0 copy.3

commit v6 on v4

--- a/solution.py
+++ b/solution.py
@@ -110,11 +110,11 @@
 
 
 CORES, YS, XS, ZS = 2, 4, 4, 8
-TOTAL = (128, 128, 320)
+TOTAL = (128, 128, 160, 160)
 HALF = tuple(t // 2 for t in TOTAL)
 FIRST = tuple(t // 8 for t in TOTAL)
 SECOND = tuple(t // 32 for t in TOTAL)
-Z_USED = (0, 0, 5)
+Z_USED = (0, 0, 5, 5)
 CHUNK = tuple(t // max(z, 1) for t, z in zip(SECOND, Z_USED))
 COPIES = 30
 
@@ -122,8 +122,9 @@
 def grouped_blocks(n):
     first = [(0, j) for j in range(n)]
     second = [(1, j) for j in range(1, n)] + [(2, 2)]
-    rest = [(i, j) for i in range(2, n) for j in range(i, n) if (i, j) != (2, 2)]
-    return first, second, rest
+    third = [(i, j) for i in (2, 3) for j in range(3, n)]
+    rest = [(i, j) for i in range(4, n) for j in range(i, n)]
+    return first, second, third, rest
 
 
 def coordinates():
@@ -196,7 +197,7 @@
             self.start(self.p_ref.at[pl.ds(self.from_p + to * size, size)], self.got1.at[s - 1], s - 1, peer)
 
     def stage1(self):
-        size, step = FIRST[self.group], 8
+        size, step = FIRST[self.group], 4
         for s in range(3):
             self.copy(self.got1.at[s], self.got1.at[s], s, self.partner).wait_recv()
 
@@ -325,8 +326,8 @@
 
 def orthonormalize_kernel(n, scale, src_ref, out_ref, *scratch):
     (own_ref, other_ref, held_hi, held_lo, p_ref, g_ref, cur_ref, d_ref, z_ref, x_ref, hi_ref, lo_ref, lane_ref) = scratch[:13]
-    groups_scratch = [scratch[13 + 5 * g : 18 + 5 * g] for g in range(3)]
-    (send, recv, x_send, x_recv, in_send, in_recv, pass_send, pass_recv, own_sem) = scratch[28:]
+    groups_scratch = [scratch[13 + 5 * g : 18 + 5 * g] for g in range(4)]
+    (send, recv, x_send, x_recv, in_send, in_recv, pass_send, pass_recv, own_sem) = scratch[33:]
     rows_each, width = src_ref.shape[0], own_ref.shape[1]
     bands = src_ref.shape[1] // width
     per_panel = B // rows_each
@@ -435,26 +436,32 @@
                         block = out[:, (j - first) * B : (j - first + 1) * B]
                         p_ref[at : at + tiles] = block.reshape(tiles, V, B)
 
-    one, two, three = (Summing(g, p_ref, g_ref, groups_scratch[g], send, recv) for g in range(3))
+    one, two, three, four = (Summing(g, p_ref, g_ref, groups_scratch[g], send, recv) for g in range(4))
     multiply(0)
     one.stage0()
     multiply(1)
     two.stage0()
     multiply(2)
     three.stage0()
+    multiply(3)
+    four.stage0()
     one.stage1()
     two.stage1()
     one.stage2()
     three.stage1()
     two.stage2()
+    four.stage1()
+    three.stage2()
     one.stage3()
-    three.stage2()
+    four.stage2()
     two.stage3()
+    three.stage3()
     one.stage5()
-    three.stage3()
+    four.stage3()
     two.stage5()
+    three.stage4()
     one.stage6()
-    three.stage4()
+    four.stage4()
     two.stage6()
     one.stage7()
     three.stage5()
@@ -510,6 +517,8 @@
                     two.stage7()
                 if k == 2:
                     three.stage7()
+                if k == 4:
+                    four.stage7()
                 prepare(k)
 
         rows = [d_ref[q * V : (q + 1) * V, :] for q in range(tiles)]
@@ -520,8 +529,11 @@
 
             @pl.when(i == k)
             def _():
+                if k == 0:
+                    four.stage5()
+                    three.stage6()
                 if k == 1:
-                    three.stage6()
+                    four.stage6()
                 panel = dot3(split(z_ref[...]), split(cur_ref[:, (k + 1) * B :]), ((1,), (0,)))
                 x_ref[k * B : (k + 1) * B, :] = panel[:, panel.shape[1] - width :]
                 for peer in range(k * per_panel, (k + 1) * per_panel):
@@ -544,7 +556,7 @@
     lax.fori_loop(0, n, step, 0)
     lax.fori_loop(1, bands, sent, 0)
     hand_over(me).wait_send()
-    for group in (one, two, three):
+    for group in (one, two, three, four):
         group.finish()
     stays.wait()
     for other in range(bands):
@@ -562,7 +574,7 @@
     tiles = lambda *shape: pltpu.VMEM((*shape, V, B), jnp.float32)
     whole = n * B + width
     summing = []
-    for g in range(3):
+    for g in range(4):
         summing += [tiles(FIRST[g]), tiles(SECOND[g]), tiles(3, FIRST[g]), tiles(3, SECOND[g])]
         summing += [tiles(ZS - 1, CHUNK[g]) if Z_USED[g] else tiles(ZS, SECOND[g])]
     return pl.pallas_call(
@@ -585,13 +597,13 @@
             pltpu.VMEM((rows, whole), jnp.bfloat16),
             pltpu.VMEM((V, B), jnp.float32),
             *summing,
-            pltpu.SemaphoreType.DMA((3 * COPIES,)),
-            pltpu.SemaphoreType.DMA((3 * COPIES,)),
+            pltpu.SemaphoreType.DMA((4 * COPIES,)),
+            pltpu.SemaphoreType.DMA((4 * COPIES,)),
             *[pltpu.SemaphoreType.DMA((bands,))] * 6,
             pltpu.SemaphoreType.DMA,
         ],
         compiler_params=pltpu.CompilerParams(
-            collective_id=0, has_side_effects=True, vmem_limit_bytes=40 << 20
+            collective_id=0, has_side_effects=True, vmem_limit_bytes=52 << 20
         ),
         name="orthonormalize",
     )(coeffs)

time: 104 us -> 97.1 us (0.934)
  Pallas kernels: 102 us -> 96 us
  local copies, waits for them, and re-layouts: 2.2 us -> 0.97 us
    pallas_call x1, Pallas kernels: 102 us -> 96 us  [orthonormalize(): pl.pallas_call(functools.partial(orthonormalize_kernel, n, 1.0 / columns_...]
    unnamed x3 -> x1, local copies, waits for them, and re-layouts: 2.2 us -> 0.97 us
where the time goes in v6:
time: 97.1 us; the launch traced here: 97 us
  Pallas kernels  96 us (99%)
    pallas_call x1, Pallas kernels, orthonormalize(): pl.pallas_call(functools.partial(orthonormalize_kernel, n, 1.0 / columns_...  96 us

profile of v6, /device:TPU:29, one launch (start us, length us, event | category | flops | bytes accessed | tf_op | source)
XLA Modules:
  0.0 97.0 jit_solution(7076178758618305678)
XLA Ops:
  0.0 96.0 %orthonormalize.1 = f32[64,4096]{1,0:T(8,128)S(1)} custom-call(f32[64,4096]{1,0:T(8,128)} %src_ref.1), custom_call_target="tpu_custom_call" | custom-call | tf_op jit(solution)/shard_map/orthonormalize/pallas_call | solution.py:580
  96.0 1.0 %copy.3 = f32[64,4096]{1,0:T(8,128)} copy(f32[64,4096]{1,0:T(8,128)S(1)} %orthonormalize.1) | data formatting | bytes 2097152

commit v7 on v6

--- a/solution.py
+++ b/solution.py
@@ -116,7 +116,8 @@
 SECOND = tuple(t // 32 for t in TOTAL)
 Z_USED = (0, 0, 5, 5)
 CHUNK = tuple(t // max(z, 1) for t, z in zip(SECOND, Z_USED))
-COPIES = 30
+COPIES = 43
+PLANE = (0,)
 
 
 def grouped_blocks(n):
@@ -190,6 +191,45 @@
         else:
             pl.when(z < Z_USED[self.group])(then)
 
+    def plane_peer(self, s):
+        core, x, y, z = self.at
+        to = lax.rem(self.a * 4 + self.b + s, 16)
+        a, b = to // 4, lax.rem(to, 4)
+        return to, device(core, jnp.where(core == 0, b, a), jnp.where(core == 0, a, b), z)
+
+    def plane_out(self):
+        size = SECOND[self.group]
+        for s in range(1, 16):
+            to, peer = self.plane_peer(s)
+            self.start(self.p_ref.at[pl.ds(self.from_p + to * size, size)], self.got1.at[s - 1], 12 + s, peer)
+
+    def plane_sum(self):
+        size = SECOND[self.group]
+        for s in range(1, 16):
+            self.copy(self.got1.at[s - 1], self.got1.at[s - 1], 12 + s, self.partner).wait_recv()
+        own = self.p_ref[pl.ds(self.from_p + (self.a * 4 + self.b) * size, size)]
+        self.acc3[...] = tree([own] + [self.got1[s] for s in range(15)])
+        self.across_z()
+
+    def plane_back(self):
+        mine = self.chunk(self.second, SECOND[self.group])
+        for s in range(1, 16):
+            to, peer = self.plane_peer(s)
+            self.start(mine, mine, 27 + s, peer)
+
+    def plane_pass(self):
+        size = SECOND[self.group]
+        for s in range(1, 16):
+            sender = lax.rem(self.a * 4 + self.b + 16 - s, 16)
+            got = self.chunk(self.half + sender * size, size)
+            self.copy(got, got, 27 + s, self.partner).wait_recv()
+        mine = self.chunk(self.half, HALF[self.group])
+        self.start(mine, mine, 0, self.partner)
+
+    def plane_done(self):
+        got = self.chunk(self.other_half, HALF[self.group])
+        self.copy(got, got, 0, self.partner).wait_recv()
+
     def stage0(self):
         size = FIRST[self.group]
         for s in (2, 1, 3):
@@ -243,7 +283,7 @@
             for s in range(1, ZS):
                 self.copy(self.acc3, self.got3.at[0], 5 + s, self.partner).wait_recv()
             self.g_ref[pl.ds(self.second, SECOND[self.group])] = tree([self.got3[k] for k in range(ZS)])
-            self.back()
+            self.plane_back() if self.group in PLANE else self.back()
             return
         size = CHUNK[self.group]
         own = self.second + self.z * size
@@ -345,7 +385,7 @@
         return carry
 
     others = [device(core, x, y, lax.rem(z + s, ZS)) for s in range(1, ZS)]
-    others += [device(core, lax.rem(x + s, XS), y, z) for s in (1, 3)]
+    others += [device(core, lax.rem(x + s, XS), lax.rem(y + t, YS), z) for s in (1, 3) for t in range(YS)]
     for peer in others:
         pl.semaphore_signal(barrier, inc=1, device_id=peer, device_id_type=MESH)
     lax.fori_loop(1, bands, greet, 0)
@@ -438,16 +478,15 @@
 
     one, two, three, four = (Summing(g, p_ref, g_ref, groups_scratch[g], send, recv) for g in range(4))
     multiply(0)
-    one.stage0()
+    one.plane_out()
     multiply(1)
     two.stage0()
     multiply(2)
     three.stage0()
     multiply(3)
     four.stage0()
-    one.stage1()
     two.stage1()
-    one.stage2()
+    one.plane_sum()
     three.stage1()
     two.stage2()
     four.stage1()
@@ -456,14 +495,13 @@
     four.stage2()
     two.stage3()
     three.stage3()
-    one.stage5()
+    two.stage5()
     four.stage3()
-    two.stage5()
     three.stage4()
-    one.stage6()
+    one.plane_pass()
     four.stage4()
     two.stage6()
-    one.stage7()
+    one.plane_done()
     three.stage5()
 
     order = [block for group in groups for block in group]
@@ -575,7 +613,7 @@
     whole = n * B + width
     summing = []
     for g in range(4):
-        summing += [tiles(FIRST[g]), tiles(SECOND[g]), tiles(3, FIRST[g]), tiles(3, SECOND[g])]
+        summing += [tiles(FIRST[g]), tiles(SECOND[g]), tiles(*((15, SECOND[g]) if g in PLANE else (3, FIRST[g]))), tiles(3, SECOND[g])]
         summing += [tiles(ZS - 1, CHUNK[g]) if Z_USED[g] else tiles(ZS, SECOND[g])]
     return pl.pallas_call(
         functools.partial(orthonormalize_kernel, n, 1.0 / columns_all),

time: 97.1 us -> 98.4 us (1.013)
  no operation moved by 1% of the time
where the time goes in v7:
time: 98.4 us; the launch traced here: 97.7 us
  Pallas kernels  96.7 us (98%)
    pallas_call x1, Pallas kernels, orthonormalize(): pl.pallas_call(functools.partial(orthonormalize_kernel, n, 1.0 / columns_...  96.7 us

profile of v7, /device:TPU:29, one launch (start us, length us, event | category | flops | bytes accessed | tf_op | source)
XLA Modules:
  0.0 97.7 jit_solution(13080558954501607498)
XLA Ops:
  0.0 96.7 %orthonormalize.1 = f32[64,4096]{1,0:T(8,128)S(1)} custom-call(f32[64,4096]{1,0:T(8,128)} %src_ref.1), custom_call_target="tpu_custom_call" | custom-call | tf_op jit(solution)/shard_map/orthonormalize/pallas_call | solution.py:618
  96.7 1.0 copy.3

commit v8 on v6

--- a/solution.py
+++ b/solution.py
@@ -114,7 +114,7 @@
 HALF = tuple(t // 2 for t in TOTAL)
 FIRST = tuple(t // 8 for t in TOTAL)
 SECOND = tuple(t // 32 for t in TOTAL)
-Z_USED = (0, 0, 5, 5)
+Z_USED = (0, 0, 0, 0)
 CHUNK = tuple(t // max(z, 1) for t, z in zip(SECOND, Z_USED))
 COPIES = 30
 
@@ -455,16 +455,15 @@
     one.stage3()
     four.stage2()
     two.stage3()
+    one.stage5()
     three.stage3()
-    one.stage5()
+    two.stage5()
     four.stage3()
-    two.stage5()
-    three.stage4()
     one.stage6()
-    four.stage4()
+    three.stage5()
     two.stage6()
     one.stage7()
-    three.stage5()
+    four.stage5()
 
     order = [block for group in groups for block in group]
     sub = lax.broadcasted_iota(jnp.int32, (V, B), 0)
@@ -530,7 +529,6 @@
             @pl.when(i == k)
             def _():
                 if k == 0:
-                    four.stage5()
                     three.stage6()
                 if k == 1:
                     four.stage6()

time: 97.1 us -> 95 us (0.978)
  Pallas kernels: 96 us -> 93.7 us
    pallas_call x1, Pallas kernels: 96 us -> 93.7 us  [orthonormalize(): pl.pallas_call(functools.partial(orthonormalize_kernel, n, 1.0 / columns_...]
where the time goes in v8:
time: 95 us; the launch traced here: 94.7 us
  Pallas kernels  93.7 us (99%)
  local copies, waits for them, and re-layouts  0.97 us (1%)
    pallas_call x1, Pallas kernels, orthonormalize(): pl.pallas_call(functools.partial(orthonormalize_kernel, n, 1.0 / columns_...  93.7 us

profile of v8, /device:TPU:29, one launch (start us, length us, event | category | flops | bytes accessed | tf_op | source)
XLA Modules:
  0.0 94.7 jit_solution(6696034840674278469)
XLA Ops:
  0.0 93.7 %orthonormalize.1 = f32[64,4096]{1,0:T(8,128)S(1)} custom-call(f32[64,4096]{1,0:T(8,128)} %src_ref.1), custom_call_target="tpu_custom_call" | custom-call | tf_op jit(solution)/shard_map/orthonormalize/pallas_call | solution.py:578
  93.8 1.0 %copy.3 = f32[64,4096]{1,0:T(8,128)} copy(f32[64,4096]{1,0:T(8,128)S(1)} %orthonormalize.1) | data formatting | bytes 2097152

commit v9 on v8

--- a/solution.py
+++ b/solution.py
@@ -325,9 +325,9 @@
 
 
 def orthonormalize_kernel(n, scale, src_ref, out_ref, *scratch):
-    (own_ref, other_ref, held_hi, held_lo, p_ref, g_ref, cur_ref, d_ref, z_ref, x_ref, hi_ref, lo_ref, lane_ref) = scratch[:13]
-    groups_scratch = [scratch[13 + 5 * g : 18 + 5 * g] for g in range(4)]
-    (send, recv, x_send, x_recv, in_send, in_recv, pass_send, pass_recv, own_sem) = scratch[33:]
+    (own_ref, other_ref, held_hi, held_lo, p_ref, g_ref, cur_ref, d_ref, z_ref, x_ref, hi_ref, lo_ref, lane_ref, row_ref) = scratch[:14]
+    groups_scratch = [scratch[14 + 5 * g : 19 + 5 * g] for g in range(4)]
+    (send, recv, x_send, x_recv, in_send, in_recv, pass_send, pass_recv, own_sem) = scratch[34:]
     rows_each, width = src_ref.shape[0], own_ref.shape[1]
     bands = src_ref.shape[1] // width
     per_panel = B // rows_each
@@ -469,12 +469,19 @@
     sub = lax.broadcasted_iota(jnp.int32, (V, B), 0)
     lane = lax.broadcasted_iota(jnp.int32, (V, B), 1)
 
-    def prepare(k):
+    def scales(k):
         at = order.index((k, k)) * tiles
         on_diagonal = [jnp.where(lane == q * V + sub, g_ref[at + q], 0.0) for q in range(tiles)]
         diagonal = jnp.sum(tree(on_diagonal), axis=0, keepdims=True)
         lanes = jnp.broadcast_to(lax.rsqrt(diagonal), (V, B))
         lane_ref[...] = lanes
+        for q in range(tiles):
+            row_ref[q * V : (q + 1) * V, :] = jnp.take_along_axis(lanes, q * V + sub, axis=1)
+
+    def prepare(k):
+        if k < 2:
+            scales(k)
+        lanes = lane_ref[...]
         taken = None
         if k:
             left = (hi_ref[: k * B, k * B : (k + 1) * B], lo_ref[: k * B, k * B : (k + 1) * B])
@@ -492,8 +499,8 @@
                 cur_ref[:, j * B : (j + 1) * B] = block
                 continue
             for q in range(tiles):
-                rows = jnp.take_along_axis(lanes, q * V + sub, axis=1)
-                d_ref[q * V : (q + 1) * V, :] = block[q * V : (q + 1) * V] * rows * lanes
+                at = slice(q * V, (q + 1) * V)
+                d_ref[at, :] = block[at] * row_ref[at, :] * lanes
 
     def remote(peer, sender):
         return pltpu.make_async_remote_copy(
@@ -516,7 +523,7 @@
                     two.stage7()
                 if k == 2:
                     three.stage7()
-                if k == 4:
+                if k == 3:
                     four.stage7()
                 prepare(k)
 
@@ -544,6 +551,8 @@
                     def _():
                         stays.start()
 
+                if 0 < k < n - 1:
+                    scales(k + 1)
                 if k < n - 1:
                     high, low = split(panel)
                     hi_ref[k * B : (k + 1) * B, (k + 1) * B :] = high
@@ -594,6 +603,7 @@
             pltpu.VMEM((rows, whole), jnp.bfloat16),
             pltpu.VMEM((rows, whole), jnp.bfloat16),
             pltpu.VMEM((V, B), jnp.float32),
+            pltpu.VMEM((B, B), jnp.float32),
             *summing,
             pltpu.SemaphoreType.DMA((4 * COPIES,)),
             pltpu.SemaphoreType.DMA((4 * COPIES,)),

time: 95 us -> 95.4 us (level)
  no operation moved by 1% of the time
where the time goes in v9:
time: 95.4 us; the launch traced here: 95.2 us
  Pallas kernels  94.2 us (99%)
  local copies, waits for them, and re-layouts  0.97 us (1%)
    pallas_call x1, Pallas kernels, orthonormalize(): pl.pallas_call(functools.partial(orthonormalize_kernel, n, 1.0 / columns_...  94.2 us

profile of v9, /device:TPU:29, one launch (start us, length us, event | category | flops | bytes accessed | tf_op | source)
XLA Modules:
  0.0 95.2 jit_solution(11269191950413837132)
XLA Ops:
  0.0 94.2 %orthonormalize.1 = f32[64,4096]{1,0:T(8,128)S(1)} custom-call(f32[64,4096]{1,0:T(8,128)} %src_ref.1), custom_call_target="tpu_custom_call" | custom-call | tf_op jit(solution)/shard_map/orthonormalize/pallas_call | solution.py:587
  94.2 1.0 %copy.3 = f32[64,4096]{1,0:T(8,128)} copy(f32[64,4096]{1,0:T(8,128)S(1)} %orthonormalize.1) | data formatting | bytes 2097152

commit v10 on v5

--- a/solution.py
+++ b/solution.py
@@ -114,7 +114,7 @@
 HALF = tuple(t // 2 for t in TOTAL)
 FIRST = tuple(t // 8 for t in TOTAL)
 SECOND = tuple(t // 32 for t in TOTAL)
-Z_USED = (0, 0, 7)
+Z_USED = (0, 0, 0)
 CHUNK = tuple(t // max(z, 1) for t, z in zip(SECOND, Z_USED))
 COPIES = 30
 
@@ -412,8 +412,8 @@
     mine.wait()
     hand_over(me).start()
     keep(own_ref, me, 0)
-    lax.fori_loop(1, bands, lambda s, carry: finish(s - 1, arrive(s, carry)), 0)
-    finish(bands - 1, 0)
+    lax.fori_loop(1, bands, arrive, 0)
+    lax.fori_loop(0, bands, finish, 0)
 
     groups = grouped_blocks(n)
 
@@ -454,7 +454,8 @@
     three.stage3()
     two.stage5()
     one.stage6()
-    three.stage4()
+    three.stage5()
+    two.stage6()
     one.stage7()
 
     order = [block for group in groups for block in group]
@@ -519,9 +520,6 @@
             @pl.when(i == k)
             def _():
                 if k == 0:
-                    two.stage6()
-                    three.stage5()
-                if k == 2:
                     three.stage6()
                 panel = dot3(split(z_ref[...]), split(cur_ref[:, (k + 1) * B :]), ((1,), (0,)))
                 x_ref[k * B : (k + 1) * B, :] = panel[:, panel.shape[1] - width :]

time: 99.2 us -> 97.8 us (0.986)
  Pallas kernels: 98.1 us -> 96.2 us
    pallas_call x1, Pallas kernels: 98.1 us -> 96.2 us  [orthonormalize(): pl.pallas_call(functools.partial(orthonormalize_kernel, n, 1.0 / columns_...]
where the time goes in v10:
time: 97.8 us; the launch traced here: 97.2 us
  Pallas kernels  96.2 us (98%)
    pallas_call x1, Pallas kernels, orthonormalize(): pl.pallas_call(functools.partial(orthonormalize_kernel, n, 1.0 / columns_...  96.2 us

profile of v10, /device:TPU:29, one launch (start us, length us, event | category | flops | bytes accessed | tf_op | source)
XLA Modules:
  0.0 97.2 jit_solution(2356529388940950433)
XLA Ops:
  0.0 96.2 %orthonormalize.1 = f32[64,4096]{1,0:T(8,128)S(1)} custom-call(f32[64,4096]{1,0:T(8,128)} %src_ref.1), custom_call_target="tpu_custom_call" | custom-call | tf_op jit(solution)/shard_map/orthonormalize/pallas_call | solution.py:567
  96.2 1.0 %copy.3 = f32[64,4096]{1,0:T(8,128)} copy(f32[64,4096]{1,0:T(8,128)S(1)} %orthonormalize.1) | data formatting | bytes 2097152

commit v11 on v8

--- a/solution.py
+++ b/solution.py
@@ -381,11 +381,8 @@
             device_id_type=MESH,
         )
 
-    def keep(ref, source, at):
-        rows = pl.ds(pl.multiple_of(source * rows_each, rows_each), rows_each)
-        high, low = split(ref[rows, :])
-        held_hi[rows, at : at + width] = high
-        held_lo[rows, at : at + width] = low
+    def keep(ref, at):
+        held_hi[:, at : at + width], held_lo[:, at : at + width] = split(ref[...])
 
     def start(s, carry):
         bring(s, me).start()
@@ -395,13 +392,11 @@
         source = lax.rem(me - s + bands, bands)
         bring(s, source).wait_recv()
         hand_over(source).start()
-        keep(own_ref, source, 0)
         return carry
 
     def finish(s, carry):
         source = lax.rem(me + 1 - 2 * core - s + bands, bands)
         hand_over(source).wait_recv()
-        keep(other_ref, source, width)
         return carry
 
     def sent(s, carry):
@@ -412,9 +407,10 @@
     lax.fori_loop(1, bands, start, 0)
     mine.wait()
     hand_over(me).start()
-    keep(own_ref, me, 0)
     lax.fori_loop(1, bands, arrive, 0)
+    keep(own_ref, 0)
     lax.fori_loop(0, bands, finish, 0)
+    keep(other_ref, width)
 
     groups = grouped_blocks(n)
 

time: 95 us -> 95.1 us (level)
  no operation moved by 1% of the time
where the time goes in v11:
time: 95.1 us; the launch traced here: 95 us
  Pallas kernels  94 us (99%)
  local copies, waits for them, and re-layouts  0.97 us (1%)
    pallas_call x1, Pallas kernels, orthonormalize(): pl.pallas_call(functools.partial(orthonormalize_kernel, n, 1.0 / columns_...  94 us

profile of v11, /device:TPU:29, one launch (start us, length us, event | category | flops | bytes accessed | tf_op | source)
XLA Modules:
  0.0 95.0 jit_solution(66431204129380763)
XLA Ops:
  0.0 94.0 %orthonormalize.1 = f32[64,4096]{1,0:T(8,128)S(1)} custom-call(f32[64,4096]{1,0:T(8,128)} %src_ref.1), custom_call_target="tpu_custom_call" | custom-call | tf_op jit(solution)/shard_map/orthonormalize/pallas_call | solution.py:574
  94.0 1.0 %copy.3 = f32[64,4096]{1,0:T(8,128)} copy(f32[64,4096]{1,0:T(8,128)S(1)} %orthonormalize.1) | data formatting | bytes 2097152

commit v12 on v8

--- a/solution.py
+++ b/solution.py
@@ -110,7 +110,7 @@
 
 
 CORES, YS, XS, ZS = 2, 4, 4, 8
-TOTAL = (128, 128, 160, 160)
+TOTAL = (128, 128, 96, 224)
 HALF = tuple(t // 2 for t in TOTAL)
 FIRST = tuple(t // 8 for t in TOTAL)
 SECOND = tuple(t // 32 for t in TOTAL)
@@ -122,8 +122,8 @@
 def grouped_blocks(n):
     first = [(0, j) for j in range(n)]
     second = [(1, j) for j in range(1, n)] + [(2, 2)]
-    third = [(i, j) for i in (2, 3) for j in range(3, n)]
-    rest = [(i, j) for i in range(4, n) for j in range(i, n)]
+    third = [(2, j) for j in range(3, n)] + [(3, 3)]
+    rest = [(i, j) for i in range(3, n) for j in range(i, n) if (i, j) != (3, 3)]
     return first, second, third, rest
 
 
@@ -516,7 +516,7 @@
                     two.stage7()
                 if k == 2:
                     three.stage7()
-                if k == 4:
+                if k == 3:
                     four.stage7()
                 prepare(k)
 

time: 95 us -> 97.3 us (1.024)
  Pallas kernels: 93.7 us -> 95.7 us
    pallas_call x1, Pallas kernels: 93.7 us -> 95.7 us  [orthonormalize(): pl.pallas_call(functools.partial(orthonormalize_kernel, n, 1.0 / columns_...]
where the time goes in v12:
time: 97.3 us; the launch traced here: 96.7 us
  Pallas kernels  95.7 us (98%)
    pallas_call x1, Pallas kernels, orthonormalize(): pl.pallas_call(functools.partial(orthonormalize_kernel, n, 1.0 / columns_...  95.7 us

profile of v12, /device:TPU:29, one launch (start us, length us, event | category | flops | bytes accessed | tf_op | source)
XLA Modules:
  0.0 96.7 jit_solution(17029963924070330829)
XLA Ops:
  0.0 95.7 %orthonormalize.1 = f32[64,4096]{1,0:T(8,128)S(1)} custom-call(f32[64,4096]{1,0:T(8,128)} %src_ref.1), custom_call_target="tpu_custom_call" | custom-call | tf_op jit(solution)/shard_map/orthonormalize/pallas_call | solution.py:578
  95.7 1.0 %copy.3 = f32[64,4096]{1,0:T(8,128)} copy(f32[64,4096]{1,0:T(8,128)S(1)} %orthonormalize.1) | data formatting | bytes 2097152

commit v13 on v9

--- a/solution.py
+++ b/solution.py
@@ -479,7 +479,7 @@
             row_ref[q * V : (q + 1) * V, :] = jnp.take_along_axis(lanes, q * V + sub, axis=1)
 
     def prepare(k):
-        if k < 2:
+        if k in (0, 1, 4):
             scales(k)
         lanes = lane_ref[...]
         taken = None
@@ -523,7 +523,7 @@
                     two.stage7()
                 if k == 2:
                     three.stage7()
-                if k == 3:
+                if k == 4:
                     four.stage7()
                 prepare(k)
 
@@ -551,7 +551,7 @@
                     def _():
                         stays.start()
 
-                if 0 < k < n - 1:
+                if 0 < k < n - 1 and k != 3:
                     scales(k + 1)
                 if k < n - 1:
                     high, low = split(panel)

time: 95.4 us -> 95.4 us (level)
  no operation moved by 1% of the time
where the time goes in v13:
time: 95.4 us; the launch traced here: 95.1 us
  Pallas kernels  94.1 us (99%)
  local copies, waits for them, and re-layouts  0.97 us (1%)
    pallas_call x1, Pallas kernels, orthonormalize(): pl.pallas_call(functools.partial(orthonormalize_kernel, n, 1.0 / columns_...  94.1 us

profile of v13, /device:TPU:29, one launch (start us, length us, event | category | flops | bytes accessed | tf_op | source)
XLA Modules:
  0.0 95.1 jit_solution(872761864246486283)
XLA Ops:
  0.0 94.1 %orthonormalize.1 = f32[64,4096]{1,0:T(8,128)S(1)} custom-call(f32[64,4096]{1,0:T(8,128)} %src_ref.1), custom_call_target="tpu_custom_call" | custom-call | tf_op jit(solution)/shard_map/orthonormalize/pallas_call | solution.py:587
  94.2 1.0 %copy.3 = f32[64,4096]{1,0:T(8,128)} copy(f32[64,4096]{1,0:T(8,128)S(1)} %orthonormalize.1) | data formatting | bytes 2097152
